TPU v7x, 128 devices: a whole 4x4x4 slice. The times are simulated.
128 devices in a mesh: ctx: 32 (over y, x, z_lo), batch: 4 (over z_hi, core).
Axes of the slice: x: 4, y: 4, z: 4 (z_hi: 2, z_lo: 2; z = z_hi * 2 + z_lo), core: 2. Of those that a mesh axis runs over, the one named last changes fastest.
Arguments:
- queries: bfloat16 [4, 8192, 2048], P('batch', 'ctx'), may hold values from -120 to 120
- keys: bfloat16 [4, 8192, 512], P('batch', 'ctx'), may hold values from -6 to 6
- values: bfloat16 [4, 8192, 512], P('batch', 'ctx'), may hold values from -6 to 6
- tau: float32 [16], replicated, may hold values from 0.5 to 2
- out_grad: bfloat16 [4, 8192, 2048], P('batch', 'ctx'), may hold values from -18 to 18
- key_blocks: int32 [4, 64, 13], replicated, may hold values from 0 to 63, as said below
Outputs:
- attended: bfloat16 [4, 8192, 2048], P('batch', 'ctx')
- query_grad: bfloat16 [4, 8192, 2048], P('batch', 'ctx')
- key_grad: bfloat16 [4, 8192, 512], P('batch', 'ctx')
- value_grad: bfloat16 [4, 8192, 512], P('batch', 'ctx')
- tau_grad: float32 [16], replicated
Inputs may be any that keep to these rules, and one draw needn't show every extreme that they name: `key_blocks`: row a of head group g lists a - 1, a, a + 1, then a + m s and a - m s for m = 1 to 5, all modulo 64, with a stride s of 2 or 3 drawn for each group and row.
All inputs are finite; a program needn't handle non-finite values.
Results may differ from a plain program's by a relative error of at most 0.0051.
Values may be sent and summed in bfloat16 or wider, within the bound.
A program may use at most 192 MiB of HBM per device.

v0:
```python
import math

import jax
import jax.numpy as jnp
from jax import lax
from jax.sharding import PartitionSpec as P

HEADS = 16
KV_HEADS = 4
HD = 128
BLOCK = 128


def passed_along(block, axis, distance):
    devices = range(lax.axis_size(axis))
    route = [((i - distance) % len(devices), i) for i in devices]
    return lax.ppermute(block, axis, route)


def body(queries, keys, values, tau, out_grad, key_blocks):
    ctx_size = lax.axis_size("ctx")
    myself = lax.axis_index("ctx")
    tokens = queries.shape[1]
    local_blocks = tokens // BLOCK
    listed_count = key_blocks.shape[2]
    block_reach = 3 * ((listed_count - 3) // 2)
    reach_dev = min((local_blocks - 1 + block_reach) // local_blocks, ctx_size // 2)
    slot_count = 2 * reach_dev + 1
    per_group = HEADS // KV_HEADS
    root_hd = math.sqrt(HD)
    paired = jnp.stack([keys[0], values[0]])
    window = jnp.zeros((2, slot_count, tokens, KV_HEADS * HD), jnp.bfloat16)
    farthest = passed_along(paired, "ctx", -reach_dev)
    window = lax.dynamic_update_slice_in_dim(window, farthest[:, None], slot_count - 1, 1)

    def walk_turn(turn_no, state_in):
        current, filled = state_in
        current = passed_along(current, "ctx", 1)
        filled = lax.dynamic_update_slice_in_dim(
            filled, current[:, None], slot_count - 1 - turn_no, 1
        )
        return (current, filled)

    window = lax.fori_loop(1, slot_count, walk_turn, (farthest, window))[1]
    blocks_all = window.reshape(2, slot_count * local_blocks, BLOCK, KV_HEADS, HD)
    own_lists = lax.dynamic_slice_in_dim(key_blocks, myself * local_blocks, local_blocks, 1)
    window_index = (
        own_lists // local_blocks - myself + reach_dev
    ) % ctx_size * local_blocks + own_lists % local_blocks
    window_ids = jnp.arange(slot_count * local_blocks, dtype=jnp.int32)
    query_all = queries[0].reshape(local_blocks, BLOCK, KV_HEADS, per_group, HD)
    grad_all = out_grad[0].reshape(local_blocks, BLOCK, KV_HEADS, per_group, HD)
    factor = tau.reshape(KV_HEADS, per_group) / root_hd
    results = []
    query_parts = []
    placed_parts = []
    scale_parts = []
    for group_id in range(KV_HEADS):
        picks = window_index[group_id].reshape(-1)
        key_rows = jnp.take(blocks_all[0, :, :, group_id], picks, axis=0).reshape(
            local_blocks, listed_count * BLOCK, HD
        )
        value_rows = jnp.take(blocks_all[1, :, :, group_id], picks, axis=0).reshape(
            local_blocks, listed_count * BLOCK, HD
        )
        query_rows = query_all[:, :, group_id]
        grad_rows = grad_all[:, :, group_id]
        scale_row = factor[group_id]
        raw_scores = jnp.einsum(
            "nqhd,nkd->nhqk", query_rows, key_rows, preferred_element_type=jnp.float32
        )
        weights = jax.nn.softmax(raw_scores * scale_row[None, :, None, None], axis=-1)
        probs_low = weights.astype(jnp.bfloat16)
        result = jnp.einsum(
            "nhqk,nkd->nqhd", probs_low, value_rows, preferred_element_type=jnp.float32
        )
        row_dot = jnp.sum(grad_rows.astype(jnp.float32) * result, axis=-1)
        dweights = jnp.einsum(
            "nqhd,nkd->nhqk", grad_rows, value_rows, preferred_element_type=jnp.float32
        )
        dscores = weights * (dweights - row_dot.transpose(0, 2, 1)[..., None])
        scale_parts.append(jnp.sum(dscores * raw_scores, axis=(0, 2, 3)) / root_hd)
        scaled = (dscores * scale_row[None, :, None, None]).astype(jnp.bfloat16)
        query_part = jnp.einsum(
            "nhqk,nkd->nqhd", scaled, key_rows, preferred_element_type=jnp.float32
        )
        key_part = jnp.einsum(
            "nhqk,nqhd->nkd", scaled, query_rows, preferred_element_type=jnp.float32
        )
        value_part = jnp.einsum(
            "nhqk,nqhd->nkd", probs_low, grad_rows, preferred_element_type=jnp.float32
        )
        chooser = (picks[:, None] == window_ids[None, :]).astype(jnp.float32)
        both_parts = jnp.stack([key_part, value_part]).reshape(
            2, local_blocks * listed_count, BLOCK * HD
        )
        placed_parts.append(
            jnp.einsum("sw,csx->cwx", chooser, both_parts, precision=lax.Precision.HIGHEST)
        )
        results.append(result)
        query_parts.append(query_part)
    attended = jnp.stack(results, axis=2).reshape(1, tokens, HEADS * HD).astype(jnp.bfloat16)
    query_grad = jnp.stack(query_parts, axis=2).reshape(1, tokens, HEADS * HD).astype(jnp.bfloat16)
    stacked = jnp.stack(placed_parts).reshape(KV_HEADS, 2, slot_count, local_blocks, BLOCK, HD)
    grads_window = stacked.transpose(2, 1, 3, 4, 0, 5).reshape(slot_count, 2, tokens, KV_HEADS * HD)

    def chain_turn(turn_no, partial_sum):
        moved = passed_along(partial_sum, "ctx", -1)
        return moved + lax.dynamic_index_in_dim(grads_window, turn_no, 0, keepdims=False)

    partial_sum = lax.fori_loop(1, slot_count, chain_turn, grads_window[0])
    summed = passed_along(partial_sum.astype(jnp.bfloat16), "ctx", reach_dev).astype(
        partial_sum.dtype
    )
    key_grad = summed[0].reshape(1, tokens, KV_HEADS * HD).astype(jnp.bfloat16)
    value_grad = summed[1].reshape(1, tokens, KV_HEADS * HD).astype(jnp.bfloat16)
    scale_total = lax.psum(jnp.stack(scale_parts), ("ctx", "batch"))
    tau_grad = scale_total.reshape(HEADS) / math.sqrt(lax.axis_size("batch") * ctx_size * tokens)
    return (attended, query_grad, key_grad, value_grad, tau_grad)


def solution(mesh):
    return jax.shard_map(
        body,
        mesh=mesh,
        in_specs=(
            P("batch", "ctx", None),
            P("batch", "ctx", None),
            P("batch", "ctx", None),
            P(),
            P("batch", "ctx", None),
            P(),
        ),
        out_specs=(
            P("batch", "ctx", None),
            P("batch", "ctx", None),
            P("batch", "ctx", None),
            P("batch", "ctx", None),
            P(),
        ),
        check_vma=False,
    )
```

profile of v0, /device:TPU:0, one launch (start us, length us, event | category | flops | bytes accessed | tf_op | source)
XLA Modules:
  0.0 1086.7 jit_solution(6687766181752277367)
XLA Ops:
  22.7 280.8 %while.30 = (s32[]{:T(128)}, bf16[2,256,512]{2,1,0:T(8,128)(2,1)}, bf16[2,17,256,512]{3,2,0,1:T(8,128)(2,1)}, s32[]{:T(128)}, s32[]{:T(128)}, /*index=5*/s32[]{:T(128)}, s32[]{:T(128)}) while((s32[]{:T(128)}, bf16[2,256,512]{2,1,0:T(8,128)(2,1)}, bf16[2,17,256,512]{3,2,0,1:T(8,128)(2,1)}, s32[]{:T(128)}, s32[]{:T(128)}, /*index=5*/s32[]{:T(128)}, ...), condition=%wide.region_1.0_spmd, body=%wide.region_0.0_spmd.sunk | while | flops 6 | bytes 4194471 | solution.py:44
  24.7 16.6 %collective-permute-done = bf16[2,256,512]{2,1,0:T(8,128)(2,1)S(1)} collective-permute-done((bf16[2,256,512]{2,1,0:T(8,128)(2,1)}, bf16[2,256,512]{2,1,0:T(8,128)(2,1)S(1)}, u32[]{:S(2)}, u32[]{:S(2)}) %collective-permute-start) | collective-permute-done | bytes 524320 | tf_op jit(solution)/shard_map/while/body/eval_jaxpr/ppermute | solution.py:17
  42.9 16.6 %collective-permute-done = bf16[2,256,512]{2,1,0:T(8,128)(2,1)S(1)} collective-permute-done((bf16[2,256,512]{2,1,0:T(8,128)(2,1)}, bf16[2,256,512]{2,1,0:T(8,128)(2,1)S(1)}, u32[]{:S(2)}, u32[]{:S(2)}) %collective-permute-start) | collective-permute-done | bytes 524320 | tf_op jit(solution)/shard_map/while/body/eval_jaxpr/ppermute | solution.py:17
  61.2 15.7 %collective-permute-done = bf16[2,256,512]{2,1,0:T(8,128)(2,1)S(1)} collective-permute-done((bf16[2,256,512]{2,1,0:T(8,128)(2,1)}, bf16[2,256,512]{2,1,0:T(8,128)(2,1)S(1)}, u32[]{:S(2)}, u32[]{:S(2)}) %collective-permute-start) | collective-permute-done | bytes 524320 | tf_op jit(solution)/shard_map/while/body/eval_jaxpr/ppermute | solution.py:17
  78.5 14.7 %collective-permute-done = bf16[2,256,512]{2,1,0:T(8,128)(2,1)S(1)} collective-permute-done((bf16[2,256,512]{2,1,0:T(8,128)(2,1)}, bf16[2,256,512]{2,1,0:T(8,128)(2,1)S(1)}, u32[]{:S(2)}, u32[]{:S(2)}) %collective-permute-start) | collective-permute-done | bytes 524320 | tf_op jit(solution)/shard_map/while/body/eval_jaxpr/ppermute | solution.py:17
  94.8 13.8 %collective-permute-done = bf16[2,256,512]{2,1,0:T(8,128)(2,1)S(1)} collective-permute-done((bf16[2,256,512]{2,1,0:T(8,128)(2,1)}, bf16[2,256,512]{2,1,0:T(8,128)(2,1)S(1)}, u32[]{:S(2)}, u32[]{:S(2)}) %collective-permute-start) | collective-permute-done | bytes 524320 | tf_op jit(solution)/shard_map/while/body/eval_jaxpr/ppermute | solution.py:17
  110.3 13.6 %collective-permute-done = bf16[2,256,512]{2,1,0:T(8,128)(2,1)S(1)} collective-permute-done((bf16[2,256,512]{2,1,0:T(8,128)(2,1)}, bf16[2,256,512]{2,1,0:T(8,128)(2,1)S(1)}, u32[]{:S(2)}, u32[]{:S(2)}) %collective-permute-start) | collective-permute-done | bytes 524320 | tf_op jit(solution)/shard_map/while/body/eval_jaxpr/ppermute | solution.py:17
  125.5 13.6 %collective-permute-done = bf16[2,256,512]{2,1,0:T(8,128)(2,1)S(1)} collective-permute-done((bf16[2,256,512]{2,1,0:T(8,128)(2,1)}, bf16[2,256,512]{2,1,0:T(8,128)(2,1)S(1)}, u32[]{:S(2)}, u32[]{:S(2)}) %collective-permute-start) | collective-permute-done | bytes 524320 | tf_op jit(solution)/shard_map/while/body/eval_jaxpr/ppermute | solution.py:17
  140.8 13.7 %collective-permute-done = bf16[2,256,512]{2,1,0:T(8,128)(2,1)S(1)} collective-permute-done((bf16[2,256,512]{2,1,0:T(8,128)(2,1)}, bf16[2,256,512]{2,1,0:T(8,128)(2,1)S(1)}, u32[]{:S(2)}, u32[]{:S(2)}) %collective-permute-start) | collective-permute-done | bytes 524320 | tf_op jit(solution)/shard_map/while/body/eval_jaxpr/ppermute | solution.py:17
  156.1 14.8 %collective-permute-done = bf16[2,256,512]{2,1,0:T(8,128)(2,1)S(1)} collective-permute-done((bf16[2,256,512]{2,1,0:T(8,128)(2,1)}, bf16[2,256,512]{2,1,0:T(8,128)(2,1)S(1)}, u32[]{:S(2)}, u32[]{:S(2)}) %collective-permute-start) | collective-permute-done | bytes 524320 | tf_op jit(solution)/shard_map/while/body/eval_jaxpr/ppermute | solution.py:17
  172.5 15.9 %collective-permute-done = bf16[2,256,512]{2,1,0:T(8,128)(2,1)S(1)} collective-permute-done((bf16[2,256,512]{2,1,0:T(8,128)(2,1)}, bf16[2,256,512]{2,1,0:T(8,128)(2,1)S(1)}, u32[]{:S(2)}, u32[]{:S(2)}) %collective-permute-start) | collective-permute-done | bytes 524320 | tf_op jit(solution)/shard_map/while/body/eval_jaxpr/ppermute | solution.py:17
  190.0 17.0 %collective-permute-done = bf16[2,256,512]{2,1,0:T(8,128)(2,1)S(1)} collective-permute-done((bf16[2,256,512]{2,1,0:T(8,128)(2,1)}, bf16[2,256,512]{2,1,0:T(8,128)(2,1)S(1)}, u32[]{:S(2)}, u32[]{:S(2)}) %collective-permute-start) | collective-permute-done | bytes 524320 | tf_op jit(solution)/shard_map/while/body/eval_jaxpr/ppermute | solution.py:17
  208.6 18.1 %collective-permute-done = bf16[2,256,512]{2,1,0:T(8,128)(2,1)S(1)} collective-permute-done((bf16[2,256,512]{2,1,0:T(8,128)(2,1)}, bf16[2,256,512]{2,1,0:T(8,128)(2,1)S(1)}, u32[]{:S(2)}, u32[]{:S(2)}) %collective-permute-start) | collective-permute-done | bytes 524320 | tf_op jit(solution)/shard_map/while/body/eval_jaxpr/ppermute | solution.py:17
  228.3 19.2 %collective-permute-done = bf16[2,256,512]{2,1,0:T(8,128)(2,1)S(1)} collective-permute-done((bf16[2,256,512]{2,1,0:T(8,128)(2,1)}, bf16[2,256,512]{2,1,0:T(8,128)(2,1)S(1)}, u32[]{:S(2)}, u32[]{:S(2)}) %collective-permute-start) | collective-permute-done | bytes 524320 | tf_op jit(solution)/shard_map/while/body/eval_jaxpr/ppermute | solution.py:17
  249.1 18.4 %collective-permute-done = bf16[2,256,512]{2,1,0:T(8,128)(2,1)S(1)} collective-permute-done((bf16[2,256,512]{2,1,0:T(8,128)(2,1)}, bf16[2,256,512]{2,1,0:T(8,128)(2,1)S(1)}, u32[]{:S(2)}, u32[]{:S(2)}) %collective-permute-start) | collective-permute-done | bytes 524320 | tf_op jit(solution)/shard_map/while/body/eval_jaxpr/ppermute | solution.py:17
  269.1 17.5 %collective-permute-done = bf16[2,256,512]{2,1,0:T(8,128)(2,1)S(1)} collective-permute-done((bf16[2,256,512]{2,1,0:T(8,128)(2,1)}, bf16[2,256,512]{2,1,0:T(8,128)(2,1)S(1)}, u32[]{:S(2)}, u32[]{:S(2)}) %collective-permute-start) | collective-permute-done | bytes 524320 | tf_op jit(solution)/shard_map/while/body/eval_jaxpr/ppermute | solution.py:17
  288.3 13.6 %collective-permute-done = bf16[2,256,512]{2,1,0:T(8,128)(2,1)S(1)} collective-permute-done((bf16[2,256,512]{2,1,0:T(8,128)(2,1)}, bf16[2,256,512]{2,1,0:T(8,128)(2,1)S(1)}, u32[]{:S(2)}, u32[]{:S(2)}) %collective-permute-start) | collective-permute-done | bytes 524320 | tf_op jit(solution)/shard_map/while/body/eval_jaxpr/ppermute | solution.py:17
  303.5 8.0 copy.85
  311.5 13.3 %reshape.174 = bf16[2,34,128,4,128]{4,3,2,1,0:T(4,128)(2,1)} reshape(bf16[2,17,256,512]{3,2,1,0:T(8,128)(2,1)} %copy.85) | data formatting | bytes 17825792 | tf_op jit(solution)/shard_map/reshape | solution.py:45
  324.9 23.1 %fusion.82 = (bf16[1,34,128,1,128]{4,3,2,1,0:T(2,128)(2,1)S(1)}, bf16[1,34,128,1,128]{4,3,2,1,0:T(2,128)(2,1)}, bf16[1,34,128,1,128]{4,3,2,1,0:T(2,128)(2,1)}, b...) fusion(bf16[2,34,128,4,128]{4,3,2,1,0:T(4,128)(2,1)} %reshape.174), kind=kLoop, calls=%fused_computation.196 | loop fusion | bytes 17825792 | tf_op jit(solution)/shard_map/slice | solution.py:60
  522.3 63.8 %psum.7 = f32[4,4]{1,0:T(4,128)S(1)} all-reduce(f32[4,4]{1,0:T(4,128)S(1)} %pad_maximum_fusion.3), channel_id=1, replica_groups=mesh['ctx'=32,'batch'=4] {'ctx','batch'}, use_global_device_ids=true, to_apply=%region_20.22 | all-reduce | flops 16 | bytes 128 | tf_op jit(solution)/shard_map/psum | solution.py:117
  614.7 6.9 copy.256
  621.6 20.0 %copy.128 = f32[17,2,2,128,4,128]{5,4,3,2,1,0:T(4,128)} copy(f32[17,2,2,128,4,128]{5,3,2,0,1,4:T(8,128)S(1)} %bitcast.371) | data formatting | bytes 35651584 | tf_op jit(solution)/shard_map/transpose | solution.py:105
  641.6 21.9 %reshape.183 = f32[17,2,256,512]{3,2,1,0:T(8,128)} reshape(f32[17,2,2,128,4,128]{5,4,3,2,1,0:T(4,128)} %copy.128) | data formatting | bytes 35651584 | tf_op jit(solution)/shard_map/reshape | solution.py:105
  665.9 406.7 %while.31 = (s32[]{:T(128)}, f32[2,256,512]{2,1,0:T(8,128)S(1)}, f32[17,2,256,512]{3,2,1,0:T(8,128)}, s32[]{:T(128)}, s32[]{:T(128)}, /*index=5*/s32[]{:T(128)}) while((s32[]{:T(128)}, f32[2,256,512]{2,1,0:T(8,128)S(1)}, f32[17,2,256,512]{3,2,1,0:T(8,128)}, s32[]{:T(128)}, s32[]{:T(128)}, /*index=5*/s32[]{:T(128)}) %tuple.109), condition=%wide.region_15.17_spmd, body=%wide.region_14.16_spmd.sunk | while | flops 262149 | bytes 7340179 | solution.py:111
  666.8 23.6 %collective-permute-done.1 = f32[2,256,512]{2,1,0:T(8,128)S(1)} collective-permute-done((f32[2,256,512]{2,1,0:T(8,128)S(1)}, f32[2,256,512]{2,1,0:T(8,128)S(1)}, u32[]{:S(2)}, u32[]{:S(2)}) %collective-permute-start.1) | collective-permute-done | bytes 1048608 | tf_op jit(solution)/shard_map/while/body/eval_jaxpr/ppermute | solution.py:17
  697.9 22.1 %collective-permute-done.1 = f32[2,256,512]{2,1,0:T(8,128)S(1)} collective-permute-done((f32[2,256,512]{2,1,0:T(8,128)S(1)}, f32[2,256,512]{2,1,0:T(8,128)S(1)}, u32[]{:S(2)}, u32[]{:S(2)}) %collective-permute-start.1) | collective-permute-done | bytes 1048608 | tf_op jit(solution)/shard_map/while/body/eval_jaxpr/ppermute | solution.py:17
  721.4 6.8 collective-permute-start.1
  728.2 21.2 %collective-permute-done.1 = f32[2,256,512]{2,1,0:T(8,128)S(1)} collective-permute-done((f32[2,256,512]{2,1,0:T(8,128)S(1)}, f32[2,256,512]{2,1,0:T(8,128)S(1)}, u32[]{:S(2)}, u32[]{:S(2)}) %collective-permute-start.1) | collective-permute-done | bytes 1048608 | tf_op jit(solution)/shard_map/while/body/eval_jaxpr/ppermute | solution.py:17
  750.8 6.8 collective-permute-start.1
  757.5 20.2 %collective-permute-done.1 = f32[2,256,512]{2,1,0:T(8,128)S(1)} collective-permute-done((f32[2,256,512]{2,1,0:T(8,128)S(1)}, f32[2,256,512]{2,1,0:T(8,128)S(1)}, u32[]{:S(2)}, u32[]{:S(2)}) %collective-permute-start.1) | collective-permute-done | bytes 1048608 | tf_op jit(solution)/shard_map/while/body/eval_jaxpr/ppermute | solution.py:17
  786.0 19.3 %collective-permute-done.1 = f32[2,256,512]{2,1,0:T(8,128)S(1)} collective-permute-done((f32[2,256,512]{2,1,0:T(8,128)S(1)}, f32[2,256,512]{2,1,0:T(8,128)S(1)}, u32[]{:S(2)}, u32[]{:S(2)}) %collective-permute-start.1) | collective-permute-done | bytes 1048608 | tf_op jit(solution)/shard_map/while/body/eval_jaxpr/ppermute | solution.py:17
  806.7 6.8 collective-permute-start.1
  813.5 18.4 %collective-permute-done.1 = f32[2,256,512]{2,1,0:T(8,128)S(1)} collective-permute-done((f32[2,256,512]{2,1,0:T(8,128)S(1)}, f32[2,256,512]{2,1,0:T(8,128)S(1)}, u32[]{:S(2)}, u32[]{:S(2)}) %collective-permute-start.1) | collective-permute-done | bytes 1048608 | tf_op jit(solution)/shard_map/while/body/eval_jaxpr/ppermute | solution.py:17
  840.1 17.5 %collective-permute-done.1 = f32[2,256,512]{2,1,0:T(8,128)S(1)} collective-permute-done((f32[2,256,512]{2,1,0:T(8,128)S(1)}, f32[2,256,512]{2,1,0:T(8,128)S(1)}, u32[]{:S(2)}, u32[]{:S(2)}) %collective-permute-start.1) | collective-permute-done | bytes 1048608 | tf_op jit(solution)/shard_map/while/body/eval_jaxpr/ppermute | solution.py:17
  865.8 16.5 %collective-permute-done.1 = f32[2,256,512]{2,1,0:T(8,128)S(1)} collective-permute-done((f32[2,256,512]{2,1,0:T(8,128)S(1)}, f32[2,256,512]{2,1,0:T(8,128)S(1)}, u32[]{:S(2)}, u32[]{:S(2)}) %collective-permute-start.1) | collective-permute-done | bytes 1048608 | tf_op jit(solution)/shard_map/while/body/eval_jaxpr/ppermute | solution.py:17
  883.8 6.8 collective-permute-start.1
  890.5 15.6 %collective-permute-done.1 = f32[2,256,512]{2,1,0:T(8,128)S(1)} collective-permute-done((f32[2,256,512]{2,1,0:T(8,128)S(1)}, f32[2,256,512]{2,1,0:T(8,128)S(1)}, u32[]{:S(2)}, u32[]{:S(2)}) %collective-permute-start.1) | collective-permute-done | bytes 1048608 | tf_op jit(solution)/shard_map/while/body/eval_jaxpr/ppermute | solution.py:17
  914.4 15.1 %collective-permute-done.1 = f32[2,256,512]{2,1,0:T(8,128)S(1)} collective-permute-done((f32[2,256,512]{2,1,0:T(8,128)S(1)}, f32[2,256,512]{2,1,0:T(8,128)S(1)}, u32[]{:S(2)}, u32[]{:S(2)}) %collective-permute-start.1) | collective-permute-done | bytes 1048608 | tf_op jit(solution)/shard_map/while/body/eval_jaxpr/ppermute | solution.py:17
  930.9 6.8 collective-permute-start.1
  937.7 15.1 %collective-permute-done.1 = f32[2,256,512]{2,1,0:T(8,128)S(1)} collective-permute-done((f32[2,256,512]{2,1,0:T(8,128)S(1)}, f32[2,256,512]{2,1,0:T(8,128)S(1)}, u32[]{:S(2)}, u32[]{:S(2)}) %collective-permute-start.1) | collective-permute-done | bytes 1048608 | tf_op jit(solution)/shard_map/while/body/eval_jaxpr/ppermute | solution.py:17
  954.3 6.8 collective-permute-start.1
  961.0 15.1 %collective-permute-done.1 = f32[2,256,512]{2,1,0:T(8,128)S(1)} collective-permute-done((f32[2,256,512]{2,1,0:T(8,128)S(1)}, f32[2,256,512]{2,1,0:T(8,128)S(1)}, u32[]{:S(2)}, u32[]{:S(2)}) %collective-permute-start.1) | collective-permute-done | bytes 1048608 | tf_op jit(solution)/shard_map/while/body/eval_jaxpr/ppermute | solution.py:17
  977.6 6.8 collective-permute-start.1
  984.4 15.5 %collective-permute-done.1 = f32[2,256,512]{2,1,0:T(8,128)S(1)} collective-permute-done((f32[2,256,512]{2,1,0:T(8,128)S(1)}, f32[2,256,512]{2,1,0:T(8,128)S(1)}, u32[]{:S(2)}, u32[]{:S(2)}) %collective-permute-start.1) | collective-permute-done | bytes 1048608 | tf_op jit(solution)/shard_map/while/body/eval_jaxpr/ppermute | solution.py:17
  1008.1 16.6 %collective-permute-done.1 = f32[2,256,512]{2,1,0:T(8,128)S(1)} collective-permute-done((f32[2,256,512]{2,1,0:T(8,128)S(1)}, f32[2,256,512]{2,1,0:T(8,128)S(1)}, u32[]{:S(2)}, u32[]{:S(2)}) %collective-permute-start.1) | collective-permute-done | bytes 1048608 | tf_op jit(solution)/shard_map/while/body/eval_jaxpr/ppermute | solution.py:17
  1032.9 17.7 %collective-permute-done.1 = f32[2,256,512]{2,1,0:T(8,128)S(1)} collective-permute-done((f32[2,256,512]{2,1,0:T(8,128)S(1)}, f32[2,256,512]{2,1,0:T(8,128)S(1)}, u32[]{:S(2)}, u32[]{:S(2)}) %collective-permute-start.1) | collective-permute-done | bytes 1048608 | tf_op jit(solution)/shard_map/while/body/eval_jaxpr/ppermute | solution.py:17
  1058.8 12.3 %collective-permute-done.1 = f32[2,256,512]{2,1,0:T(8,128)S(1)} collective-permute-done((f32[2,256,512]{2,1,0:T(8,128)S(1)}, f32[2,256,512]{2,1,0:T(8,128)S(1)}, u32[]{:S(2)}, u32[]{:S(2)}) %collective-permute-start.1) | collective-permute-done | bytes 1048608 | tf_op jit(solution)/shard_map/while/body/eval_jaxpr/ppermute | solution.py:17
  (305 shorter events, 345.8 us)
Async XLA Ops:
  0.6 10.7 copy-start.18
  2.6 14.6 %collective-permute-start.2 = (bf16[2,256,512]{2,1,0:T(8,128)(2,1)}, bf16[2,256,512]{2,1,0:T(8,128)(2,1)}, u32[]{:S(2)}, u32[]{:S(2)}) collective-permute-start(bf16[2,256,512]{2,1,0:T(8,128)(2,1)} %pad_maximum_fusion.2), channel_id=1, source_target_pairs={{32,0},{36,4},{40,8},{44,12},{48,16},{52,20},{56,24},{60,28},{64,3... | collective-permute-start | bytes 1572872 | tf_op jit(solution)/shard_map/ppermute | solution.py:17
  22.7 18.5 %collective-permute-start = (bf16[2,256,512]{2,1,0:T(8,128)(2,1)}, bf16[2,256,512]{2,1,0:T(8,128)(2,1)S(1)}, u32[]{:S(2)}, u32[]{:S(2)}) collective-permute-start(bf16[2,256,512]{2,1,0:T(8,128)(2,1)} %get-tuple-element.288), channel_id=1, source_target_pairs={{124,0},{0,4},{4,8},{8,12},{12,16},{16,20},{20,24},{24,28},{28,32}... | collective-permute-start | bytes 1572872 | tf_op jit(solution)/shard_map/while/body/eval_jaxpr/ppermute | solution.py:17
  42.9 16.6 %collective-permute-start = (bf16[2,256,512]{2,1,0:T(8,128)(2,1)}, bf16[2,256,512]{2,1,0:T(8,128)(2,1)S(1)}, u32[]{:S(2)}, u32[]{:S(2)}) collective-permute-start(bf16[2,256,512]{2,1,0:T(8,128)(2,1)} %get-tuple-element.288), channel_id=1, source_target_pairs={{124,0},{0,4},{4,8},{8,12},{12,16},{16,20},{20,24},{24,28},{28,32}... | collective-permute-start | bytes 1572872 | tf_op jit(solution)/shard_map/while/body/eval_jaxpr/ppermute | solution.py:17
  61.2 15.7 %collective-permute-start = (bf16[2,256,512]{2,1,0:T(8,128)(2,1)}, bf16[2,256,512]{2,1,0:T(8,128)(2,1)S(1)}, u32[]{:S(2)}, u32[]{:S(2)}) collective-permute-start(bf16[2,256,512]{2,1,0:T(8,128)(2,1)} %get-tuple-element.288), channel_id=1, source_target_pairs={{124,0},{0,4},{4,8},{8,12},{12,16},{16,20},{20,24},{24,28},{28,32}... | collective-permute-start | bytes 1572872 | tf_op jit(solution)/shard_map/while/body/eval_jaxpr/ppermute | solution.py:17
  78.5 14.7 %collective-permute-start = (bf16[2,256,512]{2,1,0:T(8,128)(2,1)}, bf16[2,256,512]{2,1,0:T(8,128)(2,1)S(1)}, u32[]{:S(2)}, u32[]{:S(2)}) collective-permute-start(bf16[2,256,512]{2,1,0:T(8,128)(2,1)} %get-tuple-element.288), channel_id=1, source_target_pairs={{124,0},{0,4},{4,8},{8,12},{12,16},{16,20},{20,24},{24,28},{28,32}... | collective-permute-start | bytes 1572872 | tf_op jit(solution)/shard_map/while/body/eval_jaxpr/ppermute | solution.py:17
  94.8 13.8 %collective-permute-start = (bf16[2,256,512]{2,1,0:T(8,128)(2,1)}, bf16[2,256,512]{2,1,0:T(8,128)(2,1)S(1)}, u32[]{:S(2)}, u32[]{:S(2)}) collective-permute-start(bf16[2,256,512]{2,1,0:T(8,128)(2,1)} %get-tuple-element.288), channel_id=1, source_target_pairs={{124,0},{0,4},{4,8},{8,12},{12,16},{16,20},{20,24},{24,28},{28,32}... | collective-permute-start | bytes 1572872 | tf_op jit(solution)/shard_map/while/body/eval_jaxpr/ppermute | solution.py:17
  110.3 13.6 %collective-permute-start = (bf16[2,256,512]{2,1,0:T(8,128)(2,1)}, bf16[2,256,512]{2,1,0:T(8,128)(2,1)S(1)}, u32[]{:S(2)}, u32[]{:S(2)}) collective-permute-start(bf16[2,256,512]{2,1,0:T(8,128)(2,1)} %get-tuple-element.288), channel_id=1, source_target_pairs={{124,0},{0,4},{4,8},{8,12},{12,16},{16,20},{20,24},{24,28},{28,32}... | collective-permute-start | bytes 1572872 | tf_op jit(solution)/shard_map/while/body/eval_jaxpr/ppermute | solution.py:17
  125.5 13.6 %collective-permute-start = (bf16[2,256,512]{2,1,0:T(8,128)(2,1)}, bf16[2,256,512]{2,1,0:T(8,128)(2,1)S(1)}, u32[]{:S(2)}, u32[]{:S(2)}) collective-permute-start(bf16[2,256,512]{2,1,0:T(8,128)(2,1)} %get-tuple-element.288), channel_id=1, source_target_pairs={{124,0},{0,4},{4,8},{8,12},{12,16},{16,20},{20,24},{24,28},{28,32}... | collective-permute-start | bytes 1572872 | tf_op jit(solution)/shard_map/while/body/eval_jaxpr/ppermute | solution.py:17
  140.7 13.7 %collective-permute-start = (bf16[2,256,512]{2,1,0:T(8,128)(2,1)}, bf16[2,256,512]{2,1,0:T(8,128)(2,1)S(1)}, u32[]{:S(2)}, u32[]{:S(2)}) collective-permute-start(bf16[2,256,512]{2,1,0:T(8,128)(2,1)} %get-tuple-element.288), channel_id=1, source_target_pairs={{124,0},{0,4},{4,8},{8,12},{12,16},{16,20},{20,24},{24,28},{28,32}... | collective-permute-start | bytes 1572872 | tf_op jit(solution)/shard_map/while/body/eval_jaxpr/ppermute | solution.py:17
  156.1 14.8 %collective-permute-start = (bf16[2,256,512]{2,1,0:T(8,128)(2,1)}, bf16[2,256,512]{2,1,0:T(8,128)(2,1)S(1)}, u32[]{:S(2)}, u32[]{:S(2)}) collective-permute-start(bf16[2,256,512]{2,1,0:T(8,128)(2,1)} %get-tuple-element.288), channel_id=1, source_target_pairs={{124,0},{0,4},{4,8},{8,12},{12,16},{16,20},{20,24},{24,28},{28,32}... | collective-permute-start | bytes 1572872 | tf_op jit(solution)/shard_map/while/body/eval_jaxpr/ppermute | solution.py:17
  172.5 15.9 %collective-permute-start = (bf16[2,256,512]{2,1,0:T(8,128)(2,1)}, bf16[2,256,512]{2,1,0:T(8,128)(2,1)S(1)}, u32[]{:S(2)}, u32[]{:S(2)}) collective-permute-start(bf16[2,256,512]{2,1,0:T(8,128)(2,1)} %get-tuple-element.288), channel_id=1, source_target_pairs={{124,0},{0,4},{4,8},{8,12},{12,16},{16,20},{20,24},{24,28},{28,32}... | collective-permute-start | bytes 1572872 | tf_op jit(solution)/shard_map/while/body/eval_jaxpr/ppermute | solution.py:17
  190.0 17.0 %collective-permute-start = (bf16[2,256,512]{2,1,0:T(8,128)(2,1)}, bf16[2,256,512]{2,1,0:T(8,128)(2,1)S(1)}, u32[]{:S(2)}, u32[]{:S(2)}) collective-permute-start(bf16[2,256,512]{2,1,0:T(8,128)(2,1)} %get-tuple-element.288), channel_id=1, source_target_pairs={{124,0},{0,4},{4,8},{8,12},{12,16},{16,20},{20,24},{24,28},{28,32}... | collective-permute-start | bytes 1572872 | tf_op jit(solution)/shard_map/while/body/eval_jaxpr/ppermute | solution.py:17
  208.6 18.1 %collective-permute-start = (bf16[2,256,512]{2,1,0:T(8,128)(2,1)}, bf16[2,256,512]{2,1,0:T(8,128)(2,1)S(1)}, u32[]{:S(2)}, u32[]{:S(2)}) collective-permute-start(bf16[2,256,512]{2,1,0:T(8,128)(2,1)} %get-tuple-element.288), channel_id=1, source_target_pairs={{124,0},{0,4},{4,8},{8,12},{12,16},{16,20},{20,24},{24,28},{28,32}... | collective-permute-start | bytes 1572872 | tf_op jit(solution)/shard_map/while/body/eval_jaxpr/ppermute | solution.py:17
  228.3 19.2 %collective-permute-start = (bf16[2,256,512]{2,1,0:T(8,128)(2,1)}, bf16[2,256,512]{2,1,0:T(8,128)(2,1)S(1)}, u32[]{:S(2)}, u32[]{:S(2)}) collective-permute-start(bf16[2,256,512]{2,1,0:T(8,128)(2,1)} %get-tuple-element.288), channel_id=1, source_target_pairs={{124,0},{0,4},{4,8},{8,12},{12,16},{16,20},{20,24},{24,28},{28,32}... | collective-permute-start | bytes 1572872 | tf_op jit(solution)/shard_map/while/body/eval_jaxpr/ppermute | solution.py:17
  249.1 18.4 %collective-permute-start = (bf16[2,256,512]{2,1,0:T(8,128)(2,1)}, bf16[2,256,512]{2,1,0:T(8,128)(2,1)S(1)}, u32[]{:S(2)}, u32[]{:S(2)}) collective-permute-start(bf16[2,256,512]{2,1,0:T(8,128)(2,1)} %get-tuple-element.288), channel_id=1, source_target_pairs={{124,0},{0,4},{4,8},{8,12},{12,16},{16,20},{20,24},{24,28},{28,32}... | collective-permute-start | bytes 1572872 | tf_op jit(solution)/shard_map/while/body/eval_jaxpr/ppermute | solution.py:17
  269.1 17.5 %collective-permute-start = (bf16[2,256,512]{2,1,0:T(8,128)(2,1)}, bf16[2,256,512]{2,1,0:T(8,128)(2,1)S(1)}, u32[]{:S(2)}, u32[]{:S(2)}) collective-permute-start(bf16[2,256,512]{2,1,0:T(8,128)(2,1)} %get-tuple-element.288), channel_id=1, source_target_pairs={{124,0},{0,4},{4,8},{8,12},{12,16},{16,20},{20,24},{24,28},{28,32}... | collective-permute-start | bytes 1572872 | tf_op jit(solution)/shard_map/while/body/eval_jaxpr/ppermute | solution.py:17
  288.3 13.6 %collective-permute-start = (bf16[2,256,512]{2,1,0:T(8,128)(2,1)}, bf16[2,256,512]{2,1,0:T(8,128)(2,1)S(1)}, u32[]{:S(2)}, u32[]{:S(2)}) collective-permute-start(bf16[2,256,512]{2,1,0:T(8,128)(2,1)} %get-tuple-element.288), channel_id=1, source_target_pairs={{124,0},{0,4},{4,8},{8,12},{12,16},{16,20},{20,24},{24,28},{28,32}... | collective-permute-start | bytes 1572872 | tf_op jit(solution)/shard_map/while/body/eval_jaxpr/ppermute | solution.py:17
  366.0 9.2 slice-start.6
  366.0 9.2 slice-start.12
  366.0 9.2 slice-start.7
  366.0 9.2 slice-start.13
  399.9 9.2 slice-start.8
  399.9 9.2 slice-start.14
  399.9 9.2 slice-start.9
  399.9 9.2 slice-start.15
  434.0 9.2 slice-start.10
  434.0 9.2 slice-start.16
  434.0 9.2 slice-start.11
  434.0 9.2 slice-start.17
  496.6 8.4 copy-start.14
  665.9 24.6 %collective-permute-start.1 = (f32[2,256,512]{2,1,0:T(8,128)S(1)}, f32[2,256,512]{2,1,0:T(8,128)S(1)}, u32[]{:S(2)}, u32[]{:S(2)}) collective-permute-start(f32[2,256,512]{2,1,0:T(8,128)S(1)} %get-tuple-element.308), channel_id=1, source_target_pairs={{4,0},{8,4},{12,8},{16,12},{20,16},{24,20},{28,24},{32,28},{36,32}... | collective-permute-start | bytes 3145736 | tf_op jit(solution)/shard_map/while/body/eval_jaxpr/ppermute | solution.py:17
  691.9 28.1 %collective-permute-start.1 = (f32[2,256,512]{2,1,0:T(8,128)S(1)}, f32[2,256,512]{2,1,0:T(8,128)S(1)}, u32[]{:S(2)}, u32[]{:S(2)}) collective-permute-start(f32[2,256,512]{2,1,0:T(8,128)S(1)} %get-tuple-element.308), channel_id=1, source_target_pairs={{4,0},{8,4},{12,8},{16,12},{20,16},{24,20},{28,24},{32,28},{36,32}... | collective-permute-start | bytes 3145736 | tf_op jit(solution)/shard_map/while/body/eval_jaxpr/ppermute | solution.py:17
  721.4 27.9 %collective-permute-start.1 = (f32[2,256,512]{2,1,0:T(8,128)S(1)}, f32[2,256,512]{2,1,0:T(8,128)S(1)}, u32[]{:S(2)}, u32[]{:S(2)}) collective-permute-start(f32[2,256,512]{2,1,0:T(8,128)S(1)} %get-tuple-element.308), channel_id=1, source_target_pairs={{4,0},{8,4},{12,8},{16,12},{20,16},{24,20},{28,24},{32,28},{36,32}... | collective-permute-start | bytes 3145736 | tf_op jit(solution)/shard_map/while/body/eval_jaxpr/ppermute | solution.py:17
  750.8 27.0 %collective-permute-start.1 = (f32[2,256,512]{2,1,0:T(8,128)S(1)}, f32[2,256,512]{2,1,0:T(8,128)S(1)}, u32[]{:S(2)}, u32[]{:S(2)}) collective-permute-start(f32[2,256,512]{2,1,0:T(8,128)S(1)} %get-tuple-element.308), channel_id=1, source_target_pairs={{4,0},{8,4},{12,8},{16,12},{20,16},{24,20},{28,24},{32,28},{36,32}... | collective-permute-start | bytes 3145736 | tf_op jit(solution)/shard_map/while/body/eval_jaxpr/ppermute | solution.py:17
  779.2 26.1 %collective-permute-start.1 = (f32[2,256,512]{2,1,0:T(8,128)S(1)}, f32[2,256,512]{2,1,0:T(8,128)S(1)}, u32[]{:S(2)}, u32[]{:S(2)}) collective-permute-start(f32[2,256,512]{2,1,0:T(8,128)S(1)} %get-tuple-element.308), channel_id=1, source_target_pairs={{4,0},{8,4},{12,8},{16,12},{20,16},{24,20},{28,24},{32,28},{36,32}... | collective-permute-start | bytes 3145736 | tf_op jit(solution)/shard_map/while/body/eval_jaxpr/ppermute | solution.py:17
  806.7 25.2 %collective-permute-start.1 = (f32[2,256,512]{2,1,0:T(8,128)S(1)}, f32[2,256,512]{2,1,0:T(8,128)S(1)}, u32[]{:S(2)}, u32[]{:S(2)}) collective-permute-start(f32[2,256,512]{2,1,0:T(8,128)S(1)} %get-tuple-element.308), channel_id=1, source_target_pairs={{4,0},{8,4},{12,8},{16,12},{20,16},{24,20},{28,24},{32,28},{36,32}... | collective-permute-start | bytes 3145736 | tf_op jit(solution)/shard_map/while/body/eval_jaxpr/ppermute | solution.py:17
  833.3 24.2 %collective-permute-start.1 = (f32[2,256,512]{2,1,0:T(8,128)S(1)}, f32[2,256,512]{2,1,0:T(8,128)S(1)}, u32[]{:S(2)}, u32[]{:S(2)}) collective-permute-start(f32[2,256,512]{2,1,0:T(8,128)S(1)} %get-tuple-element.308), channel_id=1, source_target_pairs={{4,0},{8,4},{12,8},{16,12},{20,16},{24,20},{28,24},{32,28},{36,32}... | collective-permute-start | bytes 3145736 | tf_op jit(solution)/shard_map/while/body/eval_jaxpr/ppermute | solution.py:17
  859.0 23.3 %collective-permute-start.1 = (f32[2,256,512]{2,1,0:T(8,128)S(1)}, f32[2,256,512]{2,1,0:T(8,128)S(1)}, u32[]{:S(2)}, u32[]{:S(2)}) collective-permute-start(f32[2,256,512]{2,1,0:T(8,128)S(1)} %get-tuple-element.308), channel_id=1, source_target_pairs={{4,0},{8,4},{12,8},{16,12},{20,16},{24,20},{28,24},{32,28},{36,32}... | collective-permute-start | bytes 3145736 | tf_op jit(solution)/shard_map/while/body/eval_jaxpr/ppermute | solution.py:17
  883.8 22.4 %collective-permute-start.1 = (f32[2,256,512]{2,1,0:T(8,128)S(1)}, f32[2,256,512]{2,1,0:T(8,128)S(1)}, u32[]{:S(2)}, u32[]{:S(2)}) collective-permute-start(f32[2,256,512]{2,1,0:T(8,128)S(1)} %get-tuple-element.308), channel_id=1, source_target_pairs={{4,0},{8,4},{12,8},{16,12},{20,16},{24,20},{28,24},{32,28},{36,32}... | collective-permute-start | bytes 3145736 | tf_op jit(solution)/shard_map/while/body/eval_jaxpr/ppermute | solution.py:17
  907.6 21.9 %collective-permute-start.1 = (f32[2,256,512]{2,1,0:T(8,128)S(1)}, f32[2,256,512]{2,1,0:T(8,128)S(1)}, u32[]{:S(2)}, u32[]{:S(2)}) collective-permute-start(f32[2,256,512]{2,1,0:T(8,128)S(1)} %get-tuple-element.308), channel_id=1, source_target_pairs={{4,0},{8,4},{12,8},{16,12},{20,16},{24,20},{28,24},{32,28},{36,32}... | collective-permute-start | bytes 3145736 | tf_op jit(solution)/shard_map/while/body/eval_jaxpr/ppermute | solution.py:17
  930.9 21.9 %collective-permute-start.1 = (f32[2,256,512]{2,1,0:T(8,128)S(1)}, f32[2,256,512]{2,1,0:T(8,128)S(1)}, u32[]{:S(2)}, u32[]{:S(2)}) collective-permute-start(f32[2,256,512]{2,1,0:T(8,128)S(1)} %get-tuple-element.308), channel_id=1, source_target_pairs={{4,0},{8,4},{12,8},{16,12},{20,16},{24,20},{28,24},{32,28},{36,32}... | collective-permute-start | bytes 3145736 | tf_op jit(solution)/shard_map/while/body/eval_jaxpr/ppermute | solution.py:17
  954.3 21.9 %collective-permute-start.1 = (f32[2,256,512]{2,1,0:T(8,128)S(1)}, f32[2,256,512]{2,1,0:T(8,128)S(1)}, u32[]{:S(2)}, u32[]{:S(2)}) collective-permute-start(f32[2,256,512]{2,1,0:T(8,128)S(1)} %get-tuple-element.308), channel_id=1, source_target_pairs={{4,0},{8,4},{12,8},{16,12},{20,16},{24,20},{28,24},{32,28},{36,32}... | collective-permute-start | bytes 3145736 | tf_op jit(solution)/shard_map/while/body/eval_jaxpr/ppermute | solution.py:17
  977.6 22.3 %collective-permute-start.1 = (f32[2,256,512]{2,1,0:T(8,128)S(1)}, f32[2,256,512]{2,1,0:T(8,128)S(1)}, u32[]{:S(2)}, u32[]{:S(2)}) collective-permute-start(f32[2,256,512]{2,1,0:T(8,128)S(1)} %get-tuple-element.308), channel_id=1, source_target_pairs={{4,0},{8,4},{12,8},{16,12},{20,16},{24,20},{28,24},{32,28},{36,32}... | collective-permute-start | bytes 3145736 | tf_op jit(solution)/shard_map/while/body/eval_jaxpr/ppermute | solution.py:17
  1001.3 23.4 %collective-permute-start.1 = (f32[2,256,512]{2,1,0:T(8,128)S(1)}, f32[2,256,512]{2,1,0:T(8,128)S(1)}, u32[]{:S(2)}, u32[]{:S(2)}) collective-permute-start(f32[2,256,512]{2,1,0:T(8,128)S(1)} %get-tuple-element.308), channel_id=1, source_target_pairs={{4,0},{8,4},{12,8},{16,12},{20,16},{24,20},{28,24},{32,28},{36,32}... | collective-permute-start | bytes 3145736 | tf_op jit(solution)/shard_map/while/body/eval_jaxpr/ppermute | solution.py:17
  1026.1 24.5 %collective-permute-start.1 = (f32[2,256,512]{2,1,0:T(8,128)S(1)}, f32[2,256,512]{2,1,0:T(8,128)S(1)}, u32[]{:S(2)}, u32[]{:S(2)}) collective-permute-start(f32[2,256,512]{2,1,0:T(8,128)S(1)} %get-tuple-element.308), channel_id=1, source_target_pairs={{4,0},{8,4},{12,8},{16,12},{20,16},{24,20},{28,24},{32,28},{36,32}... | collective-permute-start | bytes 3145736 | tf_op jit(solution)/shard_map/while/body/eval_jaxpr/ppermute | solution.py:17
  1052.0 19.1 %collective-permute-start.1 = (f32[2,256,512]{2,1,0:T(8,128)S(1)}, f32[2,256,512]{2,1,0:T(8,128)S(1)}, u32[]{:S(2)}, u32[]{:S(2)}) collective-permute-start(f32[2,256,512]{2,1,0:T(8,128)S(1)} %get-tuple-element.308), channel_id=1, source_target_pairs={{4,0},{8,4},{12,8},{16,12},{20,16},{24,20},{28,24},{32,28},{36,32}... | collective-permute-start | bytes 3145736 | tf_op jit(solution)/shard_map/while/body/eval_jaxpr/ppermute | solution.py:17
  1073.4 10.9 %collective-permute-start.3 = (bf16[2,256,512]{2,1,0:T(8,128)(2,1)}, bf16[2,256,512]{2,1,0:T(8,128)(2,1)}, u32[]{:S(2)}, u32[]{:S(2)}) collective-permute-start(bf16[2,256,512]{2,1,0:T(8,128)(2,1)} %convert_element_type.84), channel_id=1, source_target_pairs={{96,0},{100,4},{104,8},{108,12},{112,16},{116,20},{120,24},{124,28... | collective-permute-start | bytes 1572872 | tf_op jit(solution)/shard_map/ppermute | solution.py:17
  (36 other events, 145.8 us)
where the time goes:
time: 1100 us; the launch traced here: 1090 us
  waiting for transfers between devices  536 us (49%)
  local copies, waits for them, and re-layouts  211 us (19%)
  matrix products  114 us (10%)
  starting transfers between devices  107 us (10%)
  blocking collectives  63.8 us (6%)
  other arithmetic  52.3 us (5%)
    ppermute x34, waiting for transfers between devices, passed_along(): return lax.ppermute(block, axis, route)  536 us
    ppermute x34, starting transfers between devices, passed_along(): return lax.ppermute(block, axis, route)  107 us
    psum x1, blocking collectives, body(): scale_total = lax.psum(jnp.stack(scale_parts), ('ctx', 'batch'))  63.8 us
    another operation x6, local copies, waits for them, and re-layouts, body(): jnp.stack(placed_parts)  24.6 us
    dot_general x4, matrix products, body(): jnp.einsum('sw,csx->cwx', chooser, both_parts, precision=lax.Precision.HI...  24.4 us
    slice x1, local copies, waits for them, and re-layouts, body(): blocks_all[0, :, :, group_id]  23.1 us
    add x16, other arithmetic, chain_turn(): moved + lax.dynamic_index_in_dim(grads_window, turn_no, 0, keepdims=False)  22.9 us
  transfers between devices with their start and end apart: 34, of which 34 were waited for; matrix products, arithmetic and copies ran while one was open for 2% of the time, Pallas kernels for 0%

commit v1 on v0

v1 whole, which is shorter than its diff:
```python
import math

import jax
import jax.numpy as jnp
from jax import lax
from jax.experimental import pallas as pl
from jax.experimental.pallas import tpu as pltpu
from jax.sharding import PartitionSpec as P

HEADS = 16
GROUPS = 4
PER = HEADS // GROUPS
HD = 128
BLOCK = 128
WIDE = PER * HD
NY, NX, NZ = 4, 4, 2
OWN = 2
ROWS = NX * OWN
HALF = NX * OWN
PLANE = NZ * HALF
WINDOW = 3 * PLANE
f32 = jnp.float32
bf16 = jnp.bfloat16


def index_of(y, x, z):
    return (y % NY) * (NX * NZ) + (x % NX) * NZ + z % NZ


def shifted(value, dy, dx, dz):
    route = [
        (index_of(y, x, z), index_of(y + dy, x + dx, z + dz))
        for y in range(NY)
        for x in range(NX)
        for z in range(NZ)
    ]
    return lax.ppermute(value, "ctx", route)


def dot(a, b, ca, cb):
    return lax.dot_general(a, b, (((ca,), (cb,)), ((), ())), preferred_element_type=f32)


def attention_kernel(listed, table, *refs):
    qs = refs[0:NX]
    gs = refs[NX : 2 * NX]
    bundles = refs[2 * NX : 2 * NX + 6]
    scale_ref = refs[2 * NX + 6]
    outs = refs[2 * NX + 7 :]
    ods = outs[0:NX]
    fars = outs[NX : NX + 4]
    nears = outs[NX + 4 : NX + 6]
    tau_ref = outs[NX + 6]
    q_all, g_all, kw, vw, s_scr, e_scr, dk_acc, dv_acc, od, in_sem, od_sem = outs[NX + 7 :]
    r = pl.program_id(0)

    @pl.when(r == 0)
    def _():
        copies = []
        for d in range(NX):
            copies.append((qs[d], q_all.at[pl.ds(d * OWN * BLOCK, OWN * BLOCK)]))
            copies.append((gs[d], g_all.at[pl.ds(d * OWN * BLOCK, OWN * BLOCK)]))
        for i in range(6):
            copies.append((bundles[i].at[0], kw.at[pl.ds(i * HALF, HALF)]))
            copies.append((bundles[i].at[1], vw.at[pl.ds(i * HALF, HALF)]))
        started = []
        for i, (src, dst) in enumerate(copies):
            copy = pltpu.make_async_copy(src, dst, in_sem.at[i])
            copy.start()
            started.append(copy)
        dk_acc[...] = jnp.zeros_like(dk_acc)
        dv_acc[...] = jnp.zeros_like(dv_acc)
        tau_ref[...] = jnp.zeros_like(tau_ref)
        for copy in started:
            copy.wait()

    rows = pl.ds(pl.multiple_of(r * BLOCK, BLOCK), BLOCK)
    q = jnp.concatenate([q_all[rows, h * HD : (h + 1) * HD] for h in range(PER)], 0)
    g = jnp.concatenate([g_all[rows, h * HD : (h + 1) * HD] for h in range(PER)], 0)
    scale = scale_ref[0:1, :]
    high = None
    for k in range(listed):
        s = dot(kw[table[r * listed + k]], q, 1, 1)
        s_scr[k] = s
        top = s.reshape(16, 8, WIDE).max(0)
        high = top if high is None else jnp.maximum(high, top)
    high = high.max(0, keepdims=True)
    total = jnp.zeros((8, WIDE), f32)
    for k in range(listed):
        e = jnp.exp((s_scr[k] - high) * scale)
        e_scr[k] = e
        total = total + e.reshape(16, 8, WIDE).sum(0)
    inverse = 1.0 / total.sum(0, keepdims=True)
    o = None
    for k in range(listed):
        slot = table[r * listed + k]
        p = (e_scr[k] * inverse).astype(bf16)
        dv_acc[slot] += dot(p, g, 1, 0)
        part = dot(p, vw[slot], 0, 0)
        o = part if o is None else o + part
    for h in range(PER):
        od[r, 0, :, h * HD : (h + 1) * HD] = o[h * BLOCK : (h + 1) * BLOCK].astype(bf16)
    row_dot = (g.astype(f32) * o).sum(-1, keepdims=True)
    row_dot = jnp.broadcast_to(row_dot, (WIDE, HD)).T[0:1]
    tau = jnp.zeros((8, WIDE), f32)
    dq = None
    factor = inverse * scale
    for k in range(listed):
        slot = table[r * listed + k]
        t = e_scr[k] * (dot(vw[slot], g, 1, 1) - row_dot)
        tau = tau + (t * s_scr[k]).reshape(16, 8, WIDE).sum(0)
        ds = (t * factor).astype(bf16)
        dk_acc[slot] += dot(ds, q, 1, 0)
        part = dot(ds, kw[slot], 0, 0)
        dq = part if dq is None else dq + part
    for h in range(PER):
        od[r, 1, :, h * HD : (h + 1) * HD] = dq[h * BLOCK : (h + 1) * BLOCK].astype(bf16)
    tau_ref[...] += tau * inverse

    def sent(row, d):
        return pltpu.make_async_copy(od.at[row], ods[d].at[row - d * OWN], od_sem.at[row])

    for row in range(ROWS):

        @pl.when(r == row)
        def _(row=row):
            sent(row, row // OWN).start()

    @pl.when(r == ROWS - 1)
    def _():
        for kv, acc in enumerate((dk_acc, dv_acc)):
            for i in range(2):
                nears[i][kv] = acc[pl.ds(i * HALF, HALF)]
            for i in range(4):
                fars[i][kv] = acc[pl.ds(PLANE + i * HALF, HALF)].astype(bf16)
        for row in range(ROWS):
            sent(row, row // OWN).wait()


def attention(table, qs, gs, bundles, scale):
    listed = table.shape[0] // ROWS
    anywhere = pl.BlockSpec(memory_space=pl.ANY)
    half = (2, HALF, BLOCK, HD)

    def whole(shape):
        return pl.BlockSpec(shape, lambda r, *_: (0,) * len(shape))

    out_shape = (
        [jax.ShapeDtypeStruct((OWN, 2, BLOCK, WIDE), bf16)] * NX
        + [jax.ShapeDtypeStruct(half, bf16)] * 4
        + [jax.ShapeDtypeStruct(half, f32)] * 2
        + [jax.ShapeDtypeStruct((8, WIDE), f32)]
    )
    flops = ROWS * listed * BLOCK * WIDE * HD * 12
    outs = pl.pallas_call(
        lambda *refs: attention_kernel(listed, *refs),
        name="attention",
        out_shape=out_shape,
        grid_spec=pltpu.PrefetchScalarGridSpec(
            num_scalar_prefetch=1,
            grid=(ROWS,),
            in_specs=[anywhere] * (2 * NX + 6) + [whole((8, WIDE))],
            out_specs=[anywhere] * NX + [whole(half)] * 6 + [whole((8, WIDE))],
            scratch_shapes=[
                pltpu.VMEM((ROWS * BLOCK, WIDE), bf16),
                pltpu.VMEM((ROWS * BLOCK, WIDE), bf16),
                pltpu.VMEM((WINDOW, BLOCK, HD), bf16),
                pltpu.VMEM((WINDOW, BLOCK, HD), bf16),
                pltpu.VMEM((listed, BLOCK, WIDE), f32),
                pltpu.VMEM((listed, BLOCK, WIDE), f32),
                pltpu.VMEM((WINDOW, BLOCK, HD), f32),
                pltpu.VMEM((WINDOW, BLOCK, HD), f32),
                pltpu.VMEM((ROWS, 2, BLOCK, WIDE), bf16),
                pltpu.SemaphoreType.DMA((2 * NX + 12,)),
                pltpu.SemaphoreType.DMA((ROWS,)),
            ],
        ),
        compiler_params=pltpu.CompilerParams(vmem_limit_bytes=56 << 20),
        cost_estimate=pl.CostEstimate(
            flops=flops, bytes_accessed=12 << 20, transcendentals=ROWS * listed * BLOCK * WIDE
        ),
    )(table, *qs, *gs, *bundles, scale)
    return outs[:NX], outs[NX : NX + 4], outs[NX + 4 : NX + 6], outs[NX + 6]


def columns(array, place, width):
    return lax.dynamic_slice_in_dim(array, place * width, width, 1)


def side_by_side(pieces, x, width):
    rows = pieces[0].shape[0]
    whole = jnp.zeros((rows, NX * width), pieces[0].dtype)
    for d in range(NX):
        whole = lax.dynamic_update_slice(whole, pieces[d], (0, (x + d) % NX * width))
    return whole


def body(queries, keys, values, tau, out_grad, key_blocks):
    me = lax.axis_index("ctx")
    y, x, z = me // (NX * NZ), me // NZ % NX, me % NZ
    tokens = queries.shape[1]
    listed = key_blocks.shape[2]
    queries, keys, values, out_grad = queries[0], keys[0], values[0], out_grad[0]

    pieces = []
    for d in range(NX):
        to = (x + d) % NX
        pair = jnp.stack([columns(keys, to, HD), columns(values, to, HD)])
        pieces.append(pair if d == 0 else shifted(pair, 0, d, 0))
    own = jnp.stack(pieces, 1).reshape(2, HALF, BLOCK, HD)
    own, queries, out_grad = lax.optimization_barrier((own, queries, out_grad))

    below = shifted(own, 1, 0, 0)
    above = shifted(own, -1, 0, 0)
    other = shifted(own, 0, 0, 1)
    below_other = shifted(other, 1, 0, 0)
    above_other = shifted(other, -1, 0, 0)
    bundles = [own, other, below, below_other, above, above_other]

    qs, gs = [], []
    for d in range(NX):
        to = (x + d) % NX
        q, g = columns(queries, to, WIDE), columns(out_grad, to, WIDE)
        qs.append(q if d == 0 else shifted(q, 0, d, 0))
        gs.append(g if d == 0 else shifted(g, 0, d, 0))

    lists = lax.dynamic_index_in_dim(key_blocks, x, 0, keepdims=False)
    lists = lists.reshape(NY, NX, NZ, OWN, listed)
    lists = lax.dynamic_index_in_dim(lists, y, 0, keepdims=False)
    lists = lax.dynamic_index_in_dim(lists, z, 1, keepdims=False)
    lists = lists[(x - jnp.arange(NX)) % NX].reshape(-1)
    plane = (lists // 16 - y + 4) % NY
    plane = jnp.where(plane == 0, 0, jnp.where(plane == 3, 1, 2))
    far = jnp.where(lists // OWN % NZ == z, 0, 1)
    table = plane * PLANE + far * HALF + (x - lists // 4 + 64) % NX * OWN + lists % OWN

    mine = lax.dynamic_index_in_dim(tau.reshape(GROUPS, PER), x, 0, keepdims=False)
    scale = jnp.broadcast_to(jnp.repeat(mine / math.sqrt(HD), BLOCK)[None], (8, WIDE))

    ods, fars, nears, tau_part = attention(table.astype(jnp.int32), qs, gs, bundles, scale)

    below_own, below_far, above_own, above_far = fars
    far_sum = (
        nears[1] + shifted(below_far, -1, 0, 0).astype(f32) + shifted(above_far, 1, 0, 0).astype(f32)
    )
    from_other = shifted(far_sum.astype(bf16), 0, 0, 1)
    own_sum = (
        nears[0]
        + shifted(below_own, -1, 0, 0).astype(f32)
        + shifted(above_own, 1, 0, 0).astype(f32)
        + from_other.astype(f32)
    )
    done = own_sum.astype(bf16).reshape(2, NX, OWN * BLOCK, HD)
    kv_pieces = []
    od_pieces = []
    for d in range(NX):
        piece = done[:, d]
        kv_pieces.append(piece if d == 0 else shifted(piece, 0, -d, 0))
        piece = ods[d]
        od_pieces.append(piece if d == 0 else shifted(piece, 0, -d, 0))
    key_grad = side_by_side([p[0] for p in kv_pieces], x, HD)[None]
    value_grad = side_by_side([p[1] for p in kv_pieces], x, HD)[None]
    attended = side_by_side([p[:, 0].reshape(tokens, WIDE) for p in od_pieces], x, WIDE)[None]
    query_grad = side_by_side([p[:, 1].reshape(tokens, WIDE) for p in od_pieces], x, WIDE)[None]

    heads = tau_part.reshape(8, PER, BLOCK).sum((0, 2)) / math.sqrt(HD)
    placed = lax.dynamic_update_slice(jnp.zeros((GROUPS, PER), f32), heads[None], (x, 0))
    scale_total = lax.psum(placed, ("ctx", "batch"))
    count = lax.axis_size("batch") * lax.axis_size("ctx") * tokens
    tau_grad = scale_total.reshape(HEADS) / math.sqrt(count)
    return (attended, query_grad, key_grad, value_grad, tau_grad)


def solution(mesh):
    sharded = P("batch", "ctx", None)
    return jax.shard_map(
        body,
        mesh=mesh,
        in_specs=(sharded, sharded, sharded, P(), sharded, P()),
        out_specs=(sharded, sharded, sharded, sharded, P()),
        check_vma=False,
    )
```

time: 1100 us -> 233 us (0.21); the launches traced: 1090 us -> 233 us
  waiting for transfers between devices: 536 us -> 55.4 us
  local copies, waits for them, and re-layouts: 211 us -> 11 us
  matrix products: 114 us -> 0 us
  starting transfers between devices: 107 us -> 40.1 us
  other arithmetic: 52.3 us -> 2.04 us
  Pallas kernels: 0 us -> 46.5 us
  blocking collectives: 63.8 us -> 76.3 us
    ppermute x34 -> x25, waiting for transfers between devices: 536 us -> 55.4 us  [shifted(): return lax.ppermute(value, 'ctx', route)]
    dot_general x28 -> x0, matrix products: 94.7 us -> none  [the longest x4 24.4 us: body(): jnp.einsum('sw,csx->cwx', chooser, both_parts, precision=lax.Precision.HI...]
    ppermute x34 -> x25, starting transfers between devices: 107 us -> 40.1 us  [shifted(): return lax.ppermute(value, 'ctx', route)]
    another operation x22 -> x2, local copies, waits for them, and re-layouts: 47.2 us -> 0.04 us  [the longest x1 0.04 us: body(): own = jnp.stack(pieces, 1).reshape(2, HALF, BLOCK, HD)]
    pallas_call x0 -> x1, Pallas kernels: none -> 46.5 us  [attention(): pl.pallas_call(lambda *refs: attention_kernel(listed, *refs), name='atten...]
    reshape x2, local copies, waits for them, and re-layouts: 35.2 us -> 0.17 us  [the longest x1 0.08 us: body(): lists = lists[(x - jnp.arange(NX)) % NX].reshape(-1)]
    slice x12 -> x4, local copies, waits for them, and re-layouts: 29 us -> 1.17 us  [body(): p[:, 1].reshape(tokens, WIDE)]
    add x17 -> x1, other arithmetic: 23.8 us -> 0.53 us  [body(): plane * PLANE + far * HALF + (x - lists // 4 + 64) % NX * OWN + lists % OWN]
  transfers between devices with their start and end apart: 34 -> 25, of which waited for: 34 -> 16; matrix products, arithmetic and copies ran while one was open for 2% -> 3% of each run, Pallas kernels for 0% -> 0%
where the time goes in v1:
time: 233 us
  blocking collectives  76.3 us (33%)
  waiting for transfers between devices  55.4 us (24%)
  Pallas kernels  46.5 us (20%)
  starting transfers between devices  40.1 us (17%)
  local copies, waits for them, and re-layouts  11 us (5%)
    psum x1, blocking collectives, body(): scale_total = lax.psum(placed, ('ctx', 'batch'))  76.3 us
    ppermute x25, waiting for transfers between devices, shifted(): return lax.ppermute(value, 'ctx', route)  55.4 us
    pallas_call x1, Pallas kernels, attention(): pl.pallas_call(lambda *refs: attention_kernel(listed, *refs), name='atten...  46.5 us
    ppermute x25, starting transfers between devices, shifted(): return lax.ppermute(value, 'ctx', route)  40.1 us
  transfers between devices with their start and end apart: 25, of which 16 were waited for; matrix products, arithmetic and copies ran while one was open for 3% of the time, Pallas kernels for 0%

profile of v1, /device:TPU:0, one launch (start us, length us, event | category | flops | bytes accessed | tf_op | source)
XLA Modules:
  0.0 232.7 jit_solution(12752501023273061341)
XLA Ops:
  0.8 1.1 constant_dynamic-slice_fusion.15
  1.9 1.6 collective-permute-start
  3.6 2.8 %collective-permute-start.1 = (bf16[2,256,128]{2,1,0:T(8,128)(2,1)S(1)}, bf16[2,256,128]{2,1,0:T(8,128)(2,1)S(1)}, u32[]{:S(2)}, u32[]{:S(2)}) collective-permute-start(bf16[2,256,128]{2,1,0:T(8,128)(2,1)S(1)} %pad_maximum_fusion.2), channel_id=1, source_target_pairs={{0,16},{4,20},{8,24},{12,28},{16,0},{20,4},{24,8},{28,12},{32,48},... | collective-permute-start | bytes 393224 | tf_op jit(solution)/shard_map/ppermute | solution.py:37
  6.4 1.5 collective-permute-start.2
  8.3 4.0 %collective-permute-done.1 = bf16[2,256,128]{2,1,0:T(8,128)(2,1)S(1)} collective-permute-done((bf16[2,256,128]{2,1,0:T(8,128)(2,1)S(1)}, bf16[2,256,128]{2,1,0:T(8,128)(2,1)S(1)}, u32[]{:S(2)}, u32[]{:S(2)}) %collective-permute-start.1) | collective-permute-done | bytes 131104 | tf_op jit(solution)/shard_map/ppermute | solution.py:37
  12.4 2.0 collective-permute-start.9
  14.4 0.8 constant_dynamic-slice_fusion.1
  15.3 1.5 collective-permute-start.6
  16.8 2.3 collective-permute-start.7
  19.1 1.6 collective-permute-start.8
  20.7 0.8 constant_dynamic-slice_fusion.5
  22.1 5.9 %collective-permute-done.6.refs_6_ = bf16[256,512]{1,0:T(8,128)(2,1)S(1)} collective-permute-done((bf16[256,512]{1,0:T(8,128)(2,1)S(1)}, bf16[256,512]{1,0:T(8,128)(2,1)S(1)}, u32[]{:S(2)}, u32[]{:S(2)}) %collective-permute-start.6) | collective-permute-done | bytes 262176 | tf_op jit(solution)/shard_map/ppermute | solution.py:37
  28.0 1.8 collective-permute-start.4
  29.7 0.6 gather_fusion
  30.4 0.6 copy-done.10
  31.1 0.9 collective-permute-done.7.refs_7_
  32.0 1.6 collective-permute-start.10
  33.6 1.7 collective-permute-start.12
  36.0 3.0 %collective-permute-start.13 = (bf16[2,8,128,128]{3,2,1,0:T(8,128)(2,1)S(1)}, bf16[2,8,128,128]{3,2,1,0:T(8,128)(2,1)S(1)}, u32[]{:S(2)}, u32[]{:S(2)}) collective-permute-start(bf16[2,8,128,128]{3,2,1,0:T(8,128)(2,1)S(1)} %collective-permute-done.9.refs_10_), channel_id=1, source_target_pairs={{0,96},{4,100},{8,104},{12,108},{16,112},{20,116},{24,120},{28,124... | collective-permute-start | bytes 1572872 | tf_op jit(solution)/shard_map/ppermute | solution.py:37
  39.0 0.5 fusion.3.refs_0_
  39.5 1.7 collective-permute-done.4.refs_3_
  41.2 0.6 collective-permute-start.5
  41.9 5.7 %collective-permute-done.5.refs_4_ = bf16[256,512]{1,0:T(8,128)(2,1)S(1)} collective-permute-done((bf16[256,512]{1,0:T(8,128)(2,1)S(1)}, bf16[256,512]{1,0:T(8,128)(2,1)S(1)}, u32[]{:S(2)}, u32[]{:S(2)}) %collective-permute-start.5) | collective-permute-done | bytes 262176 | tf_op jit(solution)/shard_map/ppermute | solution.py:37
  47.6 0.5 collective-permute-done.10.refs_11_
  48.5 5.7 %collective-permute-done.11.refs_12_ = bf16[2,8,128,128]{3,2,1,0:T(8,128)(2,1)S(1)} collective-permute-done((bf16[2,8,128,128]{3,2,1,0:T(8,128)(2,1)S(1)}, bf16[2,8,128,128]{3,2,1,0:T(8,128)(2,1)S(1)}, u32[]{:S(2)}, u32[]{:S(2)}) %collective-permute-start.11) | collective-permute-done | bytes 524320 | tf_op jit(solution)/shard_map/ppermute | solution.py:37
  54.2 0.6 collective-permute-done.13.refs_14_
  54.8 0.6 broadcast_in_dim.54.refs_15_
  55.6 46.5 %attention.1 = (bf16[2,2,128,512]{3,2,1,0:T(8,128)(2,1)}, bf16[2,2,128,512]{3,2,1,0:T(8,128)(2,1)}, bf16[2,2,128,512]{3,2,1,0:T(8,128)(2,1)}, bf16[2,2,128,512]{...) custom-call(s32[104]{0:T(128)} %fusion.3.refs_0_, ...), custom_call_target="tpu_custom_call" | custom-call | flops 10468982784 | bytes 12582912 | tf_op jit(solution)/shard_map/attention/pallas_call | solution.py:155
  102.1 3.8 %collective-permute-start.19 = (bf16[2,8,128,128]{3,2,1,0:T(8,128)(2,1)}, bf16[2,8,128,128]{3,2,1,0:T(8,128)(2,1)S(1)}, u32[]{:S(2)}, u32[]{:S(2)}) collective-permute-start(bf16[2,8,128,128]{3,2,1,0:T(8,128)(2,1)} %get-tuple-element.30), channel_id=1, source_target_pairs={{0,96},{4,100},{8,104},{12,108},{16,112},{20,116},{24,120},{28,124... | collective-permute-start | bytes 1572872 | tf_op jit(solution)/shard_map/ppermute | solution.py:37
  105.9 3.2 %collective-permute-start.17 = (bf16[2,8,128,128]{3,2,1,0:T(8,128)(2,1)}, bf16[2,8,128,128]{3,2,1,0:T(8,128)(2,1)S(1)}, u32[]{:S(2)}, u32[]{:S(2)}) collective-permute-start(bf16[2,8,128,128]{3,2,1,0:T(8,128)(2,1)} %get-tuple-element.27), channel_id=1, source_target_pairs={{0,96},{4,100},{8,104},{12,108},{16,112},{20,116},{24,120},{28,124... | collective-permute-start | bytes 1572872 | tf_op jit(solution)/shard_map/ppermute | solution.py:37
  109.1 0.7 reduce_sum.10
  110.0 4.2 %collective-permute-start.14 = (bf16[2,2,128,512]{3,2,1,0:T(8,128)(2,1)}, bf16[2,2,128,512]{3,2,1,0:T(8,128)(2,1)S(1)}, u32[]{:S(2)}, u32[]{:S(2)}) collective-permute-start(bf16[2,2,128,512]{3,2,1,0:T(8,128)(2,1)} %get-tuple-element.23), channel_id=1, source_target_pairs={{0,24},{4,28},{8,0},{12,4},{16,8},{20,12},{24,16},{28,20},{32,56},... | collective-permute-start | bytes 1572872 | tf_op jit(solution)/shard_map/ppermute | solution.py:37
  114.2 76.3 %psum.7 = f32[4,4]{1,0:T(4,128)S(1)} all-reduce(f32[4,4]{1,0:T(4,128)S(1)} %dynamic_update_slice.83), channel_id=1, replica_groups=mesh['ctx'=32,'batch'=4] {'ctx','batch'}, use_global_device_ids=true, to_apply=%region_2.3 | all-reduce | flops 16 | bytes 128 | tf_op jit(solution)/shard_map/psum | solution.py:268
  190.6 0.6 div.79
  191.2 1.1 fusion.19
  192.6 0.9 copy-done.13
  193.6 1.9 collective-permute-start.15
  195.7 0.9 collective-permute-start.21
  196.6 13.3 %collective-permute-done.15 = bf16[2,2,128,512]{3,2,1,0:T(8,128)(2,1)S(1)} collective-permute-done((bf16[2,2,128,512]{3,2,1,0:T(8,128)(2,1)S(1)}, bf16[2,2,128,512]{3,2,1,0:T(8,128)(2,1)S(1)}, u32[]{:S(2)}, u32[]{:S(2)}) %collective-permute-start.15) | collective-permute-done | bytes 524320 | tf_op jit(solution)/shard_map/ppermute | solution.py:37
  210.0 9.6 %collective-permute-done.16 = bf16[2,2,128,512]{3,2,1,0:T(8,128)(2,1)S(1)} collective-permute-done((bf16[2,2,128,512]{3,2,1,0:T(8,128)(2,1)S(1)}, bf16[2,2,128,512]{3,2,1,0:T(8,128)(2,1)S(1)}, u32[]{:S(2)}, u32[]{:S(2)}) %collective-permute-start.16) | collective-permute-done | bytes 524320 | tf_op jit(solution)/shard_map/ppermute | solution.py:37
  219.9 1.7 copy-done.1
  222.0 0.7 collective-permute-start.22
  222.6 1.9 collective-permute-start.23
  224.5 0.7 collective-permute-start.24
  225.3 3.1 %collective-permute-done.22 = bf16[2,256,128]{2,1,0:T(8,128)(2,1)S(1)} collective-permute-done((bf16[2,256,128]{2,1,0:T(8,128)(2,1)S(1)}, bf16[2,256,128]{2,1,0:T(8,128)(2,1)S(1)}, u32[]{:S(2)}, u32[]{:S(2)}) %collective-permute-start.22) | collective-permute-done | bytes 131104 | tf_op jit(solution)/shard_map/ppermute | solution.py:37
  228.4 1.6 collective-permute-done.23
  230.1 1.7 collective-permute-done.24
  231.9 0.7 copy-done.8
  (100 shorter events, 4.2 us)
Async XLA Ops:
  0.6 7.3 %copy-start = (s32[4,64,13]{1,0,2:T(4,128)S(1)}, s32[4,64,13]{1,0,2:T(4,128)}, u32[]{:S(2)}) copy-start(s32[4,64,13]{1,0,2:T(4,128)} %param.11) | copy-start | bytes 39940
  1.9 6.4 %collective-permute-start = (bf16[2,256,128]{2,1,0:T(8,128)(2,1)S(1)}, bf16[2,256,128]{2,1,0:T(8,128)(2,1)S(1)}, u32[]{:S(2)}, u32[]{:S(2)}) collective-permute-start(bf16[2,256,128]{2,1,0:T(8,128)(2,1)S(1)} %pad_maximum_fusion.1), channel_id=1, source_target_pairs={{0,8},{4,12},{8,16},{12,20},{16,24},{20,28},{24,0},{28,4},{32,40},... | collective-permute-start | bytes 393224 | tf_op jit(solution)/shard_map/ppermute | solution.py:37
  3.6 8.7 %collective-permute-start.1 = (bf16[2,256,128]{2,1,0:T(8,128)(2,1)S(1)}, bf16[2,256,128]{2,1,0:T(8,128)(2,1)S(1)}, u32[]{:S(2)}, u32[]{:S(2)}) collective-permute-start(bf16[2,256,128]{2,1,0:T(8,128)(2,1)S(1)} %pad_maximum_fusion.2), channel_id=1, source_target_pairs={{0,16},{4,20},{8,24},{12,28},{16,0},{20,4},{24,8},{28,12},{32,48},... | collective-permute-start | bytes 393224 | tf_op jit(solution)/shard_map/ppermute | solution.py:37
  6.4 5.9 %collective-permute-start.2 = (bf16[2,256,128]{2,1,0:T(8,128)(2,1)S(1)}, bf16[2,256,128]{2,1,0:T(8,128)(2,1)S(1)}, u32[]{:S(2)}, u32[]{:S(2)}) collective-permute-start(bf16[2,256,128]{2,1,0:T(8,128)(2,1)S(1)} %pad_maximum_fusion.3), channel_id=1, source_target_pairs={{0,24},{4,28},{8,0},{12,4},{16,8},{20,12},{24,16},{28,20},{32,56},... | collective-permute-start | bytes 393224 | tf_op jit(solution)/shard_map/ppermute | solution.py:37
  12.3 2.1 copy-start.2
  12.4 21.2 %copy-start.7 = (bf16[2,4,256,128]{3,2,1,0:T(8,128)(2,1)}, bf16[2,4,256,128]{3,2,1,0:T(8,128)(2,1)S(1)}, u32[]{:S(2)}) copy-start(bf16[2,4,256,128]{3,2,1,0:T(8,128)(2,1)S(1)} %copy.21) | copy-start | bytes 1572868
  12.4 8.2 %copy-start.3 = (bf16[1,256,2048]{2,1,0:T(8,128)(2,1)S(1)}, bf16[1,256,2048]{2,1,0:T(8,128)(2,1)}, u32[]{:S(2)}) copy-start(bf16[1,256,2048]{2,1,0:T(8,128)(2,1)} %param.6) | copy-start | bytes 3145732
  12.4 22.9 %collective-permute-start.9 = (bf16[2,8,128,128]{3,2,1,0:T(8,128)(2,1)S(1)}, bf16[2,8,128,128]{3,2,1,0:T(8,128)(2,1)S(1)}, u32[]{:S(2)}, u32[]{:S(2)}) collective-permute-start(bf16[2,8,128,128]{3,2,1,0:T(8,128)(2,1)S(1)} %bitcast.63), channel_id=1, source_target_pairs={{0,4},{4,0},{8,12},{12,8},{16,20},{20,16},{24,28},{28,24},{32,36},... | collective-permute-start | bytes 1572872 | tf_op jit(solution)/shard_map/ppermute | solution.py:37
  15.3 12.7 %collective-permute-start.6 = (bf16[256,512]{1,0:T(8,128)(2,1)S(1)}, bf16[256,512]{1,0:T(8,128)(2,1)S(1)}, u32[]{:S(2)}, u32[]{:S(2)}) collective-permute-start(bf16[256,512]{1,0:T(8,128)(2,1)S(1)} %get-tuple-element.35), channel_id=1, source_target_pairs={{0,8},{4,12},{8,16},{12,20},{16,24},{20,28},{24,0},{28,4},{32,40},... | collective-permute-start | bytes 786440 | tf_op jit(solution)/shard_map/ppermute | solution.py:37
  16.8 15.2 %collective-permute-start.7 = (bf16[256,512]{1,0:T(8,128)(2,1)S(1)}, bf16[256,512]{1,0:T(8,128)(2,1)S(1)}, u32[]{:S(2)}, u32[]{:S(2)}) collective-permute-start(bf16[256,512]{1,0:T(8,128)(2,1)S(1)} %get-tuple-element.34), channel_id=1, source_target_pairs={{0,16},{4,20},{8,24},{12,28},{16,0},{20,4},{24,8},{28,12},{32,48},... | collective-permute-start | bytes 786440 | tf_op jit(solution)/shard_map/ppermute | solution.py:37
  19.1 14.5 %collective-permute-start.8 = (bf16[256,512]{1,0:T(8,128)(2,1)S(1)}, bf16[256,512]{1,0:T(8,128)(2,1)S(1)}, u32[]{:S(2)}, u32[]{:S(2)}) collective-permute-start(bf16[256,512]{1,0:T(8,128)(2,1)S(1)} %get-tuple-element.33), channel_id=1, source_target_pairs={{0,24},{4,28},{8,0},{12,4},{16,8},{20,12},{24,16},{28,20},{32,56},... | collective-permute-start | bytes 786440 | tf_op jit(solution)/shard_map/ppermute | solution.py:37
  21.5 14.5 %collective-permute-start.3 = (bf16[256,512]{1,0:T(8,128)(2,1)S(1)}, bf16[256,512]{1,0:T(8,128)(2,1)}, u32[]{:S(2)}, u32[]{:S(2)}) collective-permute-start(bf16[256,512]{1,0:T(8,128)(2,1)S(1)} %get-tuple-element.39), channel_id=1, source_target_pairs={{0,8},{4,12},{8,16},{12,20},{16,24},{20,28},{24,0},{28,4},{32,40},... | collective-permute-start | bytes 786440 | tf_op jit(solution)/shard_map/ppermute | solution.py:37
  28.0 27.4 %copy-start.18 = (bf16[256,512]{1,0:T(8,128)(2,1)}, bf16[256,512]{1,0:T(8,128)(2,1)S(1)}, u32[]{:S(2)}) copy-start(bf16[256,512]{1,0:T(8,128)(2,1)S(1)} %collective-permute-done.6.refs_6_) | copy-start | bytes 786436
  28.0 13.2 %collective-permute-start.4 = (bf16[256,512]{1,0:T(8,128)(2,1)S(1)}, bf16[256,512]{1,0:T(8,128)(2,1)}, u32[]{:S(2)}, u32[]{:S(2)}) collective-permute-start(bf16[256,512]{1,0:T(8,128)(2,1)S(1)} %get-tuple-element.38), channel_id=1, source_target_pairs={{0,16},{4,20},{8,24},{12,28},{16,0},{20,4},{24,8},{28,12},{32,48},... | collective-permute-start | bytes 786440 | tf_op jit(solution)/shard_map/ppermute | solution.py:37
  30.3 0.7 copy-start.10
  32.0 23.4 %copy-start.19 = (bf16[256,512]{1,0:T(8,128)(2,1)}, bf16[256,512]{1,0:T(8,128)(2,1)S(1)}, u32[]{:S(2)}) copy-start(bf16[256,512]{1,0:T(8,128)(2,1)S(1)} %collective-permute-done.7.refs_7_) | copy-start | bytes 786436
  32.0 16.1 %collective-permute-start.10 = (bf16[2,8,128,128]{3,2,1,0:T(8,128)(2,1)S(1)}, bf16[2,8,128,128]{3,2,1,0:T(8,128)(2,1)S(1)}, u32[]{:S(2)}, u32[]{:S(2)}) collective-permute-start(bf16[2,8,128,128]{3,2,1,0:T(8,128)(2,1)S(1)} %bitcast.64), channel_id=1, source_target_pairs={{0,32},{4,36},{8,40},{12,44},{16,48},{20,52},{24,56},{28,60},{32,6... | collective-permute-start | bytes 1572872 | tf_op jit(solution)/shard_map/ppermute | solution.py:37
  33.6 21.8 %copy-start.20 = (bf16[256,512]{1,0:T(8,128)(2,1)}, bf16[256,512]{1,0:T(8,128)(2,1)S(1)}, u32[]{:S(2)}) copy-start(bf16[256,512]{1,0:T(8,128)(2,1)S(1)} %collective-permute-done.8.refs_8_) | copy-start | bytes 786436
  33.6 14.9 %collective-permute-start.12 = (bf16[2,8,128,128]{3,2,1,0:T(8,128)(2,1)S(1)}, bf16[2,8,128,128]{3,2,1,0:T(8,128)(2,1)S(1)}, u32[]{:S(2)}, u32[]{:S(2)}) collective-permute-start(bf16[2,8,128,128]{3,2,1,0:T(8,128)(2,1)S(1)} %bitcast.65), channel_id=1, source_target_pairs={{0,96},{4,100},{8,104},{12,108},{16,112},{20,116},{24,120},{28,124... | collective-permute-start | bytes 1572872 | tf_op jit(solution)/shard_map/ppermute | solution.py:37
  35.3 20.1 %copy-start.11 = (bf16[2,8,128,128]{3,2,1,0:T(8,128)(2,1)}, bf16[2,8,128,128]{3,2,1,0:T(8,128)(2,1)S(1)}, u32[]{:S(2)}) copy-start(bf16[2,8,128,128]{3,2,1,0:T(8,128)(2,1)S(1)} %collective-permute-done.9.refs_10_) | copy-start | bytes 1572868
  35.3 18.9 %collective-permute-start.11 = (bf16[2,8,128,128]{3,2,1,0:T(8,128)(2,1)S(1)}, bf16[2,8,128,128]{3,2,1,0:T(8,128)(2,1)S(1)}, u32[]{:S(2)}, u32[]{:S(2)}) collective-permute-start(bf16[2,8,128,128]{3,2,1,0:T(8,128)(2,1)S(1)} %collective-permute-done.9.refs_10_), channel_id=1, source_target_pairs={{0,32},{4,36},{8,40},{12,44},{16,48},{20,52},{24,56},{28,60},{32,6... | collective-permute-start | bytes 1572872 | tf_op jit(solution)/shard_map/ppermute | solution.py:37
  36.0 18.8 %collective-permute-start.13 = (bf16[2,8,128,128]{3,2,1,0:T(8,128)(2,1)S(1)}, bf16[2,8,128,128]{3,2,1,0:T(8,128)(2,1)S(1)}, u32[]{:S(2)}, u32[]{:S(2)}) collective-permute-start(bf16[2,8,128,128]{3,2,1,0:T(8,128)(2,1)S(1)} %collective-permute-done.9.refs_10_), channel_id=1, source_target_pairs={{0,96},{4,100},{8,104},{12,108},{16,112},{20,116},{24,120},{28,124... | collective-permute-start | bytes 1572872 | tf_op jit(solution)/shard_map/ppermute | solution.py:37
  41.2 6.4 %collective-permute-start.5 = (bf16[256,512]{1,0:T(8,128)(2,1)S(1)}, bf16[256,512]{1,0:T(8,128)(2,1)S(1)}, u32[]{:S(2)}, u32[]{:S(2)}) collective-permute-start(bf16[256,512]{1,0:T(8,128)(2,1)S(1)} %get-tuple-element.37), channel_id=1, source_target_pairs={{0,24},{4,28},{8,0},{12,4},{16,8},{20,12},{24,16},{28,20},{32,56},... | collective-permute-start | bytes 786440 | tf_op jit(solution)/shard_map/ppermute | solution.py:37
  47.6 7.8 %copy-start.21 = (bf16[256,512]{1,0:T(8,128)(2,1)}, bf16[256,512]{1,0:T(8,128)(2,1)S(1)}, u32[]{:S(2)}) copy-start(bf16[256,512]{1,0:T(8,128)(2,1)S(1)} %collective-permute-done.5.refs_4_) | copy-start | bytes 786436
  48.1 7.4 %copy-start.14 = (bf16[2,8,128,128]{3,2,1,0:T(8,128)(2,1)}, bf16[2,8,128,128]{3,2,1,0:T(8,128)(2,1)S(1)}, u32[]{:S(2)}) copy-start(bf16[2,8,128,128]{3,2,1,0:T(8,128)(2,1)S(1)} %collective-permute-done.10.refs_11_) | copy-start | bytes 1572868
  48.5 6.9 %copy-start.15 = (bf16[2,8,128,128]{3,2,1,0:T(8,128)(2,1)}, bf16[2,8,128,128]{3,2,1,0:T(8,128)(2,1)S(1)}, u32[]{:S(2)}) copy-start(bf16[2,8,128,128]{3,2,1,0:T(8,128)(2,1)S(1)} %collective-permute-done.12.refs_13_) | copy-start | bytes 1572868
  54.2 1.3 copy-start.16
  54.8 0.8 copy-start.17
  102.1 90.5 %collective-permute-start.19 = (bf16[2,8,128,128]{3,2,1,0:T(8,128)(2,1)}, bf16[2,8,128,128]{3,2,1,0:T(8,128)(2,1)S(1)}, u32[]{:S(2)}, u32[]{:S(2)}) collective-permute-start(bf16[2,8,128,128]{3,2,1,0:T(8,128)(2,1)} %get-tuple-element.30), channel_id=1, source_target_pairs={{0,96},{4,100},{8,104},{12,108},{16,112},{20,116},{24,120},{28,124... | collective-permute-start | bytes 1572872 | tf_op jit(solution)/shard_map/ppermute | solution.py:37
  105.9 89.6 %collective-permute-start.20 = (bf16[2,8,128,128]{3,2,1,0:T(8,128)(2,1)}, bf16[2,8,128,128]{3,2,1,0:T(8,128)(2,1)S(1)}, u32[]{:S(2)}, u32[]{:S(2)}) collective-permute-start(bf16[2,8,128,128]{3,2,1,0:T(8,128)(2,1)} %get-tuple-element.31), channel_id=1, source_target_pairs={{0,32},{4,36},{8,40},{12,44},{16,48},{20,52},{24,56},{28,60},{32,6... | collective-permute-start | bytes 1572872 | tf_op jit(solution)/shard_map/ppermute | solution.py:37
  105.9 114.0 %collective-permute-start.17 = (bf16[2,8,128,128]{3,2,1,0:T(8,128)(2,1)}, bf16[2,8,128,128]{3,2,1,0:T(8,128)(2,1)S(1)}, u32[]{:S(2)}, u32[]{:S(2)}) collective-permute-start(bf16[2,8,128,128]{3,2,1,0:T(8,128)(2,1)} %get-tuple-element.27), channel_id=1, source_target_pairs={{0,96},{4,100},{8,104},{12,108},{16,112},{20,116},{24,120},{28,124... | collective-permute-start | bytes 1572872 | tf_op jit(solution)/shard_map/ppermute | solution.py:37
  109.1 110.8 %collective-permute-start.18 = (bf16[2,8,128,128]{3,2,1,0:T(8,128)(2,1)}, bf16[2,8,128,128]{3,2,1,0:T(8,128)(2,1)S(1)}, u32[]{:S(2)}, u32[]{:S(2)}) collective-permute-start(bf16[2,8,128,128]{3,2,1,0:T(8,128)(2,1)} %get-tuple-element.28), channel_id=1, source_target_pairs={{0,32},{4,36},{8,40},{12,44},{16,48},{20,52},{24,56},{28,60},{32,6... | collective-permute-start | bytes 1572872 | tf_op jit(solution)/shard_map/ppermute | solution.py:37
  110.0 85.7 %collective-permute-start.14 = (bf16[2,2,128,512]{3,2,1,0:T(8,128)(2,1)}, bf16[2,2,128,512]{3,2,1,0:T(8,128)(2,1)S(1)}, u32[]{:S(2)}, u32[]{:S(2)}) collective-permute-start(bf16[2,2,128,512]{3,2,1,0:T(8,128)(2,1)} %get-tuple-element.23), channel_id=1, source_target_pairs={{0,24},{4,28},{8,0},{12,4},{16,8},{20,12},{24,16},{28,20},{32,56},... | collective-permute-start | bytes 1572872 | tf_op jit(solution)/shard_map/ppermute | solution.py:37
  192.4 3.1 %copy-start.4 = (f32[2,8,128,128]{3,2,1,0:T(8,128)S(1)}, f32[2,8,128,128]{3,2,1,0:T(8,128)}, u32[]{:S(2)}) copy-start(f32[2,8,128,128]{3,2,1,0:T(8,128)} %get-tuple-element.29) | copy-start | bytes 3145732
  192.4 1.1 copy-start.13
  192.6 2.9 %copy-start.12 = (bf16[2,2,128,512]{3,2,1,0:T(8,128)(2,1)S(1)}, bf16[2,2,128,512]{3,2,1,0:T(8,128)(2,1)}, u32[]{:S(2)}) copy-start(bf16[2,2,128,512]{3,2,1,0:T(8,128)(2,1)} %get-tuple-element.25) | copy-start | bytes 1572868
  193.6 16.4 %collective-permute-start.15 = (bf16[2,2,128,512]{3,2,1,0:T(8,128)(2,1)S(1)}, bf16[2,2,128,512]{3,2,1,0:T(8,128)(2,1)S(1)}, u32[]{:S(2)}, u32[]{:S(2)}) collective-permute-start(bf16[2,2,128,512]{3,2,1,0:T(8,128)(2,1)S(1)} %copy-done.13), channel_id=1, source_target_pairs={{0,16},{4,20},{8,24},{12,28},{16,0},{20,4},{24,8},{28,12},{32,48},... | collective-permute-start | bytes 1572872 | tf_op jit(solution)/shard_map/ppermute | solution.py:37
  195.4 24.2 %collective-permute-start.16 = (bf16[2,2,128,512]{3,2,1,0:T(8,128)(2,1)S(1)}, bf16[2,2,128,512]{3,2,1,0:T(8,128)(2,1)S(1)}, u32[]{:S(2)}, u32[]{:S(2)}) collective-permute-start(bf16[2,2,128,512]{3,2,1,0:T(8,128)(2,1)S(1)} %copy-done.12), channel_id=1, source_target_pairs={{0,8},{4,12},{8,16},{12,20},{16,24},{20,28},{24,0},{28,4},{32,40},... | collective-permute-start | bytes 1572872 | tf_op jit(solution)/shard_map/ppermute | solution.py:37
  195.7 24.2 %collective-permute-start.21 = (bf16[2,8,128,128]{3,2,1,0:T(8,128)(2,1)S(1)}, bf16[2,8,128,128]{3,2,1,0:T(8,128)(2,1)S(1)}, u32[]{:S(2)}, u32[]{:S(2)}) collective-permute-start(bf16[2,8,128,128]{3,2,1,0:T(8,128)(2,1)S(1)} %add_convert_fusion.1), channel_id=1, source_target_pairs={{0,4},{4,0},{8,12},{12,8},{16,20},{20,16},{24,28},{28,24},{32,36},... | collective-permute-start | bytes 1572872 | tf_op jit(solution)/shard_map/ppermute | solution.py:37
  219.7 1.9 copy-start.1
  219.7 2.1 copy-start.6
  219.9 2.0 copy-start.5
  222.0 6.4 %collective-permute-start.22 = (bf16[2,256,128]{2,1,0:T(8,128)(2,1)S(1)}, bf16[2,256,128]{2,1,0:T(8,128)(2,1)S(1)}, u32[]{:S(2)}, u32[]{:S(2)}) collective-permute-start(bf16[2,256,128]{2,1,0:T(8,128)(2,1)S(1)} %get-tuple-element.43), channel_id=1, source_target_pairs={{0,24},{4,28},{8,0},{12,4},{16,8},{20,12},{24,16},{28,20},{32,56},... | collective-permute-start | bytes 393224 | tf_op jit(solution)/shard_map/ppermute | solution.py:37
  222.6 7.4 %collective-permute-start.23 = (bf16[2,256,128]{2,1,0:T(8,128)(2,1)S(1)}, bf16[2,256,128]{2,1,0:T(8,128)(2,1)S(1)}, u32[]{:S(2)}, u32[]{:S(2)}) collective-permute-start(bf16[2,256,128]{2,1,0:T(8,128)(2,1)S(1)} %get-tuple-element.42), channel_id=1, source_target_pairs={{0,16},{4,20},{8,24},{12,28},{16,0},{20,4},{24,8},{28,12},{32,48},... | collective-permute-start | bytes 393224 | tf_op jit(solution)/shard_map/ppermute | solution.py:37
  224.5 7.3 %collective-permute-start.24 = (bf16[2,256,128]{2,1,0:T(8,128)(2,1)S(1)}, bf16[2,256,128]{2,1,0:T(8,128)(2,1)S(1)}, u32[]{:S(2)}, u32[]{:S(2)}) collective-permute-start(bf16[2,256,128]{2,1,0:T(8,128)(2,1)S(1)} %get-tuple-element.41), channel_id=1, source_target_pairs={{0,8},{4,12},{8,16},{12,20},{16,24},{20,28},{24,0},{28,4},{32,40},... | collective-permute-start | bytes 393224 | tf_op jit(solution)/shard_map/ppermute | solution.py:37
  231.9 0.7 copy-start.8
  231.9 0.8 copy-start.9

commit v2 on v0

v2 whole, which is shorter than its diff:
```python
import math

import jax
import jax.numpy as jnp
from jax import lax
from jax.experimental import pallas as pl
from jax.experimental.pallas import tpu as pltpu
from jax.sharding import PartitionSpec as P

HEADS = 16
GROUPS = 4
PER = HEADS // GROUPS
HD = 128
BLOCK = 128
BLOCKS = 64
WIDE = PER * HD
NY, NX, NZ = 4, 4, 2
OWN = 2
ROWS = NX * OWN
HALF = NX * OWN
PLANE = NZ * HALF
WINDOW = 3 * PLANE
TOKENS = OWN * BLOCK
FIXED = (-1, 0, 1, 6, -6)
EITHER = ((2, 3), (-2, -3), (4, 9), (-4, -9), (8, 12), (-8, -12), (10, 15), (-10, -15))
LISTED = len(FIXED) + len(EITHER)
f32 = jnp.float32
bf16 = jnp.bfloat16
MESH = pl.DeviceIdType.MESH
BATCH = 4


def index_of(y, x, z):
    return lax.rem(y + NY, NY) * (NX * NZ) + lax.rem(x + NX, NX) * NZ + lax.rem(z, NZ)


def dot(a, b, ca, cb):
    return lax.dot_general(a, b, (((ca,), (cb,)), ((), ())), preferred_element_type=f32)


def kernel(
    key_blocks, tau_ref, queries, keys, values, grads,
    attended, query_grad, key_grad, value_grad, tau_out,
    kw, vw, q_all, g_all, s_all, high_all, e_scr, dk_acc, dv_acc, od,
    stage, arrived, z_stage, z_arrived, final, tau_acc, tau_x, tau_y, tau_z,
    here_sem, in_send, in_recv, od_send, od_recv, out_send, out_recv, tau_send, tau_recv,
):
    me = lax.axis_index("ctx")
    batch = lax.axis_index("batch")
    y, x, z = me // (NX * NZ), lax.rem(me // NZ, NX), lax.rem(me, NZ)

    def at(dy, dx, dz):
        return {"ctx": index_of(y + dy, x + dx, z + dz)}

    def far(dz, db):
        return {"ctx": index_of(y, x, z + dz), "batch": lax.rem(batch + db, BATCH)}

    def remote(src, dst, send, recv, device):
        return pltpu.make_async_remote_copy(
            src_ref=src, dst_ref=dst, send_sem=send, recv_sem=recv,
            device_id=device, device_id_type=MESH,
        )

    near_half = PLANE + z * HALF
    other_half = PLANE + (1 - z) * HALF

    def columns(array, n, place, width):
        return array.at[n, :, pl.ds(pl.multiple_of(place * width, width), width)]

    here_k, here_v, here_q, here_g = [
        [
            pltpu.make_async_copy(columns(array, n, x, width), place(0, n), here_sem.at[2 * i + n])
            for n in range(OWN)
        ]
        for i, (array, width, place) in enumerate(
            (
                (keys, HD, lambda d, n: kw.at[near_half + x * OWN + n]),
                (values, HD, lambda d, n: vw.at[near_half + x * OWN + n]),
                (queries, WIDE, lambda d, n: q_all.at[d * OWN + n]),
                (grads, WIDE, lambda d, n: g_all.at[d * OWN + n]),
            )
        )
    ]
    here = here_k + here_v + here_q + here_g
    for copy in here:
        copy.start()

    partners = [at(0, d, 0) for d in (1, 2, 3)] + [at(d, 0, 0) for d in (1, 2, 3)]
    partners += [far(dz, db) for dz in range(NZ) for db in range(BATCH) if dz or db]
    barrier = pltpu.get_barrier_semaphore()
    for device in partners:
        pl.semaphore_signal(barrier, inc=1, device_id=device, device_id_type=MESH)
    pl.semaphore_wait(barrier, len(partners))

    def along_x(array, width, place, first):
        out = []
        for d in (1, 2, 3):
            to = lax.rem(x + d, NX)
            for n in range(OWN):
                i = first + (d - 1) * OWN + n
                out.append(
                    remote(columns(array, n, to, width), place(d, n), in_send.at[i], in_recv.at[i], at(0, d, 0))
                )
        return out

    k_x = along_x(keys, HD, lambda d, n: kw.at[near_half + x * OWN + n], 0)
    v_x = along_x(values, HD, lambda d, n: vw.at[near_half + x * OWN + n], 6)
    q_x = along_x(queries, WIDE, lambda d, n: q_all.at[d * OWN + n], 12)
    g_x = along_x(grads, WIDE, lambda d, n: g_all.at[d * OWN + n], 18)

    def plane_sends(window, n):
        own = [
            remote(window.at[pl.ds(near_half, HALF)], window.at[pl.ds(near_half, HALF)], in_send.at[n], in_recv.at[n], at(0, 0, 1)),
            remote(window.at[pl.ds(near_half, HALF)], window.at[pl.ds(near_half - PLANE, HALF)], in_send.at[n + 1], in_recv.at[n + 1], at(1, 0, 0)),
            remote(window.at[pl.ds(near_half, HALF)], window.at[pl.ds(near_half + PLANE, HALF)], in_send.at[n + 2], in_recv.at[n + 2], at(3, 0, 0)),
        ]
        other = [
            remote(window.at[pl.ds(other_half, HALF)], window.at[pl.ds(other_half - PLANE, HALF)], in_send.at[n + 3], in_recv.at[n + 3], at(1, 0, 0)),
            remote(window.at[pl.ds(other_half, HALF)], window.at[pl.ds(other_half + PLANE, HALF)], in_send.at[n + 4], in_recv.at[n + 4], at(3, 0, 0)),
        ]
        return own, other

    k_own, k_other = plane_sends(kw, 24)
    v_own, v_other = plane_sends(vw, 29)

    def start(copies):
        for copy in copies:
            copy.start()

    def received(copies):
        for copy in copies:
            copy.wait_recv()

    start(k_x)
    start(v_x)
    for copy in here_k:
        copy.wait()
    received(k_x)
    start(k_own)
    for copy in here_v:
        copy.wait()
    received(v_x)
    start(q_x)
    received(k_own[:1])
    start(k_other)
    start(v_own)
    start(g_x)

    dk_acc[...] = jnp.zeros_like(dk_acc)
    dv_acc[...] = jnp.zeros_like(dv_acc)
    tau_acc[...] = jnp.zeros_like(tau_acc)
    scale = jnp.concatenate(
        [jnp.full((1, BLOCK), tau_ref[x * PER + h] / math.sqrt(HD), f32) for h in range(PER)], 1
    )

    def row_place(r):
        return lax.rem(x - r // OWN + NX, NX) * (NZ * OWN) + z * OWN + lax.rem(r, OWN)

    def slot_of(linear):
        rest = lax.rem(linear, PLANE)
        return (linear // PLANE) * PLANE + lax.rem(rest // OWN, NZ) * HALF + (rest // (NZ * OWN)) * OWN + lax.rem(rest, OWN)

    def is_two(r):
        a = y * PLANE + row_place(r)
        sought = lax.rem(a + 2, BLOCKS)
        hit = 0
        for k in range(LISTED):
            hit = jnp.where(key_blocks[x, a, k] == sought, 1, hit)
        return hit

    def slots(r):
        linear = PLANE + row_place(r)
        return (
            [slot_of(linear + o) for o in FIXED],
            [(slot_of(linear + two), slot_of(linear + three)) for two, three in EITHER],
        )

    def listed_slots(fixed, either, two):
        return fixed + [jnp.where(two == 1, p, q) for p, q in either]

    def heads_of(array, r):
        return jnp.concatenate([array[r, :, h * HD : (h + 1) * HD] for h in range(PER)], 0)

    def scores(r, _):
        q = heads_of(q_all, r)
        picks = listed_slots(*slots(r), is_two(r))
        high = None
        for k, slot in enumerate(picks):
            s = dot(kw[slot], q, 1, 1)
            s_all[r, k] = s
            top = s.reshape(16, 8, WIDE).max(0)
            high = top if high is None else jnp.maximum(high, top)
        high_all[r] = high
        return 0

    for copy in here_q:
        copy.wait()
    received(q_x)
    received(k_own[1:])
    received(k_other)
    lax.fori_loop(0, ROWS // 2, scores, 0)
    received(v_own[:1])
    start(v_other)
    lax.fori_loop(ROWS // 2, ROWS, scores, 0)
    for copy in here_g:
        copy.wait()
    received(g_x)
    received(v_own[1:])
    received(v_other)

    def back(r, which, out, local):
        d, half = r // OWN, lax.rem(r, OWN)
        dst = columns(out, half, x, WIDE)
        n = which * ROWS + r
        if local:
            return pltpu.make_async_copy(od.at[r, which], dst, od_recv.at[n])
        return remote(od.at[r, which], dst, od_send.at[n], od_recv.at[n], at(0, NX - d, 0))

    def send_back(r, which, out):
        @pl.when(r < OWN)
        def _():
            back(r, which, out, True).start()

        @pl.when(r >= OWN)
        def _():
            back(r, which, out, False).start()

    def row(step, _):
        r = lax.rem(step + OWN, ROWS)
        q = heads_of(q_all, r)
        g = heads_of(g_all, r)
        fixed, either = slots(r)
        two = is_two(r)
        picks = listed_slots(fixed, either, two)
        weight = two.astype(f32)

        def add(acc, k, part):
            if k < len(FIXED):
                acc[fixed[k]] += part
            else:
                p, q = either[k - len(FIXED)]
                acc[p] += part * weight
                acc[q] += part * (1.0 - weight)

        high = high_all[r].max(0, keepdims=True)
        total = jnp.zeros((8, WIDE), f32)
        for k in range(LISTED):
            e = jnp.exp((s_all[r, k] - high) * scale)
            e_scr[k] = e
            total = total + e.reshape(16, 8, WIDE).sum(0)
        inverse = 1.0 / total.sum(0, keepdims=True)
        o = None
        for k in range(LISTED):
            p = (e_scr[k] * inverse).astype(bf16)
            add(dv_acc, k, dot(p, g, 1, 0))
            part = dot(p, vw[picks[k]], 0, 0)
            o = part if o is None else o + part
        for h in range(PER):
            od[r, 0, :, h * HD : (h + 1) * HD] = o[h * BLOCK : (h + 1) * BLOCK].astype(bf16)
        send_back(r, 0, attended)
        row_dot = (g.astype(f32) * o).sum(-1, keepdims=True)
        row_dot = jnp.broadcast_to(row_dot, (WIDE, HD)).T[0:1]
        tau = jnp.zeros((8, WIDE), f32)
        dq = None
        factor = inverse * scale
        for k in range(LISTED):
            t = e_scr[k] * (dot(vw[picks[k]], g, 1, 1) - row_dot)
            tau = tau + (t * s_all[r, k]).reshape(16, 8, WIDE).sum(0)
            ds = (t * factor).astype(bf16)
            add(dk_acc, k, dot(ds, q, 1, 0))
            part = dot(ds, kw[picks[k]], 0, 0)
            dq = part if dq is None else dq + part
        for h in range(PER):
            od[r, 1, :, h * HD : (h + 1) * HD] = dq[h * BLOCK : (h + 1) * BLOCK].astype(bf16)
        send_back(r, 1, query_grad)
        tau_acc[...] += tau * inverse
        return 0

    lax.fori_loop(0, ROWS, row, 0)

    accs = (dv_acc, dk_acc)
    y_out = []
    for kv in range(2):
        for half in range(2):
            for side in range(2):
                n = kv * 4 + half * 2 + side
                begin = side * 2 * PLANE + (1 - z if half == 0 else z) * HALF
                stage[n] = accs[kv][pl.ds(begin, HALF)].astype(bf16)
                copy = remote(stage.at[n], arrived.at[n], out_send.at[n], out_recv.at[n], at(3 if side == 0 else 1, 0, 0))
                copy.start()
                y_out.append(copy)

    tau_waits = []
    parts = jnp.concatenate([tau_acc[:, h * BLOCK : (h + 1) * BLOCK].sum(0, keepdims=True) for h in range(PER)], 0)
    tau_x[x] = jnp.concatenate([parts, jnp.zeros_like(parts)], 0)
    tau_first = [remote(tau_x.at[x], tau_x.at[x], tau_send.at[d - 1], tau_recv.at[d - 1], at(0, d, 0)) for d in (1, 2, 3)]
    start(tau_first)
    received(tau_first)
    tau_y[y] = tau_x[...]
    tau_second = [remote(tau_y.at[y], tau_y.at[y], tau_send.at[d + 2], tau_recv.at[d + 2], at(d, 0, 0)) for d in (1, 2, 3)]
    start(tau_second)

    z_out = []
    for kv in range(2):
        received(y_out[kv * 4 : kv * 4 + 2])
        summed = accs[kv][pl.ds(other_half, HALF)] + arrived[kv * 4].astype(f32) + arrived[kv * 4 + 1].astype(f32)
        z_stage[kv] = summed.astype(bf16)
        copy = remote(z_stage.at[kv], z_arrived.at[kv], out_send.at[8 + kv], out_recv.at[8 + kv], at(0, 0, 1))
        copy.start()
        z_out.append(copy)

    received(tau_second)
    spot = z * BATCH + batch
    tau_z[spot] = tau_y[0] + tau_y[1] + tau_y[2] + tau_y[3]
    tau_third = []
    for dz in range(NZ):
        for db in range(BATCH):
            if dz or db:
                n = 6 + len(tau_third)
                tau_third.append(remote(tau_z.at[spot], tau_z.at[spot], tau_send.at[n], tau_recv.at[n], far(dz, db)))
    start(tau_third)

    x_out = []
    x_local = []
    for kv, out in enumerate((value_grad, key_grad)):
        received(y_out[kv * 4 + 2 : kv * 4 + 4])
        received(z_out[kv : kv + 1])
        summed = accs[kv][pl.ds(near_half, HALF)] + arrived[kv * 4 + 2].astype(f32) + arrived[kv * 4 + 3].astype(f32)
        final[kv] = (summed + z_arrived[kv].astype(f32)).astype(bf16)
        for d in range(NX):
            from_x = lax.rem(x - d + NX, NX)
            for m in range(OWN):
                src = final.at[kv, from_x * OWN + m]
                dst = columns(out, m, x, HD)
                n = 10 + (kv * NX + d) * OWN + m
                if d == 0:
                    copy = pltpu.make_async_copy(src, dst, out_recv.at[n])
                    x_local.append(copy)
                else:
                    copy = remote(src, dst, out_send.at[n], out_recv.at[n], at(0, NX - d, 0))
                    x_out.append(copy)
                copy.start()

    received(tau_third)
    whole = tau_z[0]
    for n in range(1, NZ * BATCH):
        whole = whole + tau_z[n]
    norm = math.sqrt(HD) * math.sqrt(BATCH * NY * NX * NZ * TOKENS)
    for n in range(NX):
        for h in range(PER):
            tau_out[n * PER + h] = jnp.sum(whole[n, h : h + 1, :]) / norm

    received(x_out)
    for copy in x_local:
        copy.wait()
    for which, out in enumerate((attended, query_grad)):
        for r in range(ROWS):
            back(r, which, out, r < OWN).wait()
    for copy in k_x + v_x + q_x + g_x + k_own + k_other + v_own + v_other:
        copy.wait_send()
    for copy in y_out + z_out + x_out + tau_first + tau_second + tau_third:
        copy.wait_send()


def body(queries, keys, values, tau, out_grad, key_blocks):
    anywhere = pl.BlockSpec(memory_space=pl.ANY)
    scalars = pl.BlockSpec(memory_space=pltpu.SMEM)
    shape = lambda a: (OWN, BLOCK, a.shape[2])
    half = (HALF, BLOCK, HD)
    blocked = [a.reshape(shape(a)) for a in (queries, keys, values, out_grad)]
    outs = pl.pallas_call(
        kernel,
        name="attention",
        out_shape=(
            jax.ShapeDtypeStruct(shape(queries), bf16),
            jax.ShapeDtypeStruct(shape(queries), bf16),
            jax.ShapeDtypeStruct(shape(keys), bf16),
            jax.ShapeDtypeStruct(shape(keys), bf16),
            jax.ShapeDtypeStruct((HEADS,), f32),
        ),
        in_specs=[scalars, scalars] + [anywhere] * 4,
        out_specs=(anywhere,) * 4 + (scalars,),
        scratch_shapes=[
            pltpu.VMEM((WINDOW, BLOCK, HD), bf16),
            pltpu.VMEM((WINDOW, BLOCK, HD), bf16),
            pltpu.VMEM((ROWS, BLOCK, WIDE), bf16),
            pltpu.VMEM((ROWS, BLOCK, WIDE), bf16),
            pltpu.VMEM((ROWS, LISTED, BLOCK, WIDE), f32),
            pltpu.VMEM((ROWS, 8, WIDE), f32),
            pltpu.VMEM((LISTED, BLOCK, WIDE), f32),
            pltpu.VMEM((WINDOW, BLOCK, HD), f32),
            pltpu.VMEM((WINDOW, BLOCK, HD), f32),
            pltpu.VMEM((ROWS, 2, BLOCK, WIDE), bf16),
            pltpu.VMEM((8,) + half, bf16),
            pltpu.VMEM((8,) + half, bf16),
            pltpu.VMEM((2,) + half, bf16),
            pltpu.VMEM((2,) + half, bf16),
            pltpu.VMEM((2,) + half, bf16),
            pltpu.VMEM((8, WIDE), f32),
            pltpu.VMEM((NX, 8, BLOCK), f32),
            pltpu.VMEM((NY, NX, 8, BLOCK), f32),
            pltpu.VMEM((NZ * BATCH, NX, 8, BLOCK), f32),
            pltpu.SemaphoreType.DMA((8,)),
            pltpu.SemaphoreType.DMA((34,)),
            pltpu.SemaphoreType.DMA((34,)),
            pltpu.SemaphoreType.DMA((2 * ROWS,)),
            pltpu.SemaphoreType.DMA((2 * ROWS,)),
            pltpu.SemaphoreType.DMA((26,)),
            pltpu.SemaphoreType.DMA((26,)),
            pltpu.SemaphoreType.DMA((13,)),
            pltpu.SemaphoreType.DMA((13,)),
        ],
        compiler_params=pltpu.CompilerParams(
            collective_id=0, has_side_effects=True, vmem_limit_bytes=62 << 20
        ),
    )(key_blocks, tau, *blocked)
    return tuple(o.reshape(a.shape) for o, a in zip(outs[:4], (queries, queries, keys, keys))) + (outs[4],)


def solution(mesh):
    sharded = P("batch", "ctx", None)
    return jax.shard_map(
        body,
        mesh=mesh,
        in_specs=(sharded, sharded, sharded, P(), sharded, P()),
        out_specs=(sharded, sharded, sharded, sharded, P()),
        check_vma=False,
    )
```

time: 1100 us -> 121 us (0.11); the launches traced: 1090 us -> 121 us
  waiting for transfers between devices: 536 us -> 0 us
  local copies, waits for them, and re-layouts: 211 us -> 7.26 us
  matrix products: 114 us -> 0 us
  Pallas kernels: 0 us -> 113 us
  starting transfers between devices: 107 us -> 0 us
  blocking collectives: 63.8 us -> 0 us
  other arithmetic: 52.3 us -> 0 us
    ppermute x34 -> x0, waiting for transfers between devices: 536 us -> none  [passed_along(): return lax.ppermute(block, axis, route)]
    pallas_call x0 -> x1, Pallas kernels: none -> 113 us  [body(): pl.pallas_call(kernel, name='attention', out_shape=(jax.ShapeDtypeStruct(...]
    ppermute x34 -> x0, starting transfers between devices: 107 us -> none  [passed_along(): return lax.ppermute(block, axis, route)]
    dot_general x28 -> x0, matrix products: 94.7 us -> none  [the longest x4 24.4 us: body(): jnp.einsum('sw,csx->cwx', chooser, both_parts, precision=lax.Precision.HI...]
    psum x1 -> x0, blocking collectives: 63.8 us -> none  [body(): scale_total = lax.psum(jnp.stack(scale_parts), ('ctx', 'batch'))]
    another operation x22 -> x0, local copies, waits for them, and re-layouts: 47.2 us -> none  [the longest x6 24.6 us: body(): jnp.stack(placed_parts)]
    reshape x2 -> x0, local copies, waits for them, and re-layouts: 35.2 us -> none  [the longest x1 21.9 us: body(): stacked.transpose(2, 1, 3, 4, 0, 5)]
    slice x12 -> x0, local copies, waits for them, and re-layouts: 29 us -> none  [the longest x1 23.1 us: body(): blocks_all[0, :, :, group_id]]
  transfers between devices with their start and end apart: 34 -> 0, of which waited for: 34 -> 0; matrix products, arithmetic and copies ran while one was open for 2% -> 0% of each run, Pallas kernels for 0% -> 0%
where the time goes in v2:
time: 121 us
  Pallas kernels  113 us (93%)
  local copies, waits for them, and re-layouts  7.26 us (6%)
    pallas_call x1, Pallas kernels, body(): pl.pallas_call(kernel, name='attention', out_shape=(jax.ShapeDtypeStruct(...  113 us
    unnamed x14, local copies, waits for them, and re-layouts  7.26 us

profile of v2, /device:TPU:0, one launch (start us, length us, event | category | flops | bytes accessed | tf_op | source)
XLA Modules:
  0.0 120.8 jit_solution(6352328372997784087)
XLA Ops:
  0.6 1.5 %copy.11.key_blocks = s32[4,64,13]{2,1,0:T(8,128)} copy(s32[4,64,13]{1,0,2:T(4,128)} %param.11) | data formatting | bytes 26624 | tf_op args[5]
  2.1 112.9 %attention.1 = (bf16[2,128,2048]{2,1,0:T(8,128)(2,1)}, bf16[2,128,2048]{2,1,0:T(8,128)(2,1)}, bf16[2,128,512]{2,1,0:T(8,128)(2,1)}, bf16[2,128,512]{2,1,0:T(8,128)(2,1)}, f32[16]{0:T(128)}) custom-call(s32[4,64,13]{2,1,0:T(8,128)} %copy.11.key_blocks, f32[16]{0:T(128)} %tau_ref.1, bf16[2,128,2048]{2,1,0:T(8,128)(2,1)} %bitcast.8, ...), custom_call_target="tpu_custom_call" | custom-call | tf_op jit(solution)/shard_map/attention/pallas_call | solution.py:371
  115.0 0.0 copy-start
  115.0 2.4 %copy.17 = bf16[1,256,2048]{2,1,0:T(8,128)(2,1)} copy(bf16[1,256,2048]{2,1,0:T(8,128)(2,1)} %bitcast.11) | data formatting | bytes 2097152
  117.4 0.0 copy-done
  117.4 0.0 copy-start.2
  117.4 1.0 copy.18
  118.4 0.1 copy-done.2
  118.5 0.0 copy-start.1
  118.5 0.7 copy.19
  119.2 0.3 copy-done.1
  119.6 0.0 copy-start.3
  119.6 0.7 copy.20
  120.3 0.0 copy-done.3
  120.3 0.5 copy.21
Async XLA Ops:
  115.0 2.4 %copy-start = (bf16[2,128,2048]{2,1,0:T(8,128)(2,1)S(1)}, bf16[2,128,2048]{2,1,0:T(8,128)(2,1)}, u32[]{:S(2)}) copy-start(bf16[2,128,2048]{2,1,0:T(8,128)(2,1)} %get-tuple-element.11) | copy-start | bytes 3145732
  117.4 1.1 copy-start.2
  118.5 1.0 copy-start.1
  119.6 0.7 copy-start.3

commit v3 on v2

--- a/solution.py
+++ b/solution.py
@@ -26,6 +26,7 @@
 LISTED = len(FIXED) + len(EITHER)
 f32 = jnp.float32
 bf16 = jnp.bfloat16
+LOG2E = math.log2(math.e)
 MESH = pl.DeviceIdType.MESH
 BATCH = 4
 
@@ -41,7 +42,7 @@
 def kernel(
     key_blocks, tau_ref, queries, keys, values, grads,
     attended, query_grad, key_grad, value_grad, tau_out,
-    kw, vw, q_all, g_all, s_all, high_all, e_scr, dk_acc, dv_acc, od,
+    kw, vw, q_all, g_all, s_all, ds_all, shift_all, dot_all, dk_acc, dv_acc, od,
     stage, arrived, z_stage, z_arrived, final, tau_acc, tau_x, tau_y, tau_z,
     here_sem, in_send, in_recv, od_send, od_recv, out_send, out_recv, tau_send, tau_recv,
 ):
@@ -131,27 +132,34 @@
         for copy in copies:
             copy.wait_recv()
 
+    def wait(copies):
+        for copy in copies:
+            copy.wait()
+
+    q_even, q_odd = q_x[0::OWN], q_x[1::OWN]
     start(k_x)
-    start(v_x)
-    for copy in here_k:
-        copy.wait()
-    received(k_x)
-    start(k_own)
-    for copy in here_v:
-        copy.wait()
-    received(v_x)
-    start(q_x)
-    received(k_own[:1])
-    start(k_other)
-    start(v_own)
-    start(g_x)
-
     dk_acc[...] = jnp.zeros_like(dk_acc)
     dv_acc[...] = jnp.zeros_like(dv_acc)
-    tau_acc[...] = jnp.zeros_like(tau_acc)
     scale = jnp.concatenate(
         [jnp.full((1, BLOCK), tau_ref[x * PER + h] / math.sqrt(HD), f32) for h in range(PER)], 1
     )
+    scale_two = scale * LOG2E
+    wait(here_k)
+    received(k_x)
+    start(k_own)
+    start(q_even)
+    start(v_x)
+    received(k_own[:1])
+    start(k_other)
+    wait(here_v)
+    received(q_even)
+    received(v_x)
+    start(v_own[:1])
+    start(q_odd)
+    wait(here_q)
+    received(k_own[1:])
+    received(k_other)
+    start(v_own[1:])
 
     def row_place(r):
         return lax.rem(x - r // OWN + NX, NX) * (NZ * OWN) + z * OWN + lax.rem(r, OWN)
@@ -165,45 +173,72 @@
         sought = lax.rem(a + 2, BLOCKS)
         hit = 0
         for k in range(LISTED):
-            hit = jnp.where(key_blocks[x, a, k] == sought, 1, hit)
+            hit = jnp.where(key_blocks[k, x, a] == sought, 1, hit)
         return hit
 
     def slots(r):
         linear = PLANE + row_place(r)
-        return (
-            [slot_of(linear + o) for o in FIXED],
-            [(slot_of(linear + two), slot_of(linear + three)) for two, three in EITHER],
-        )
-
-    def listed_slots(fixed, either, two):
-        return fixed + [jnp.where(two == 1, p, q) for p, q in either]
+        fixed = [slot_of(linear + o) for o in FIXED]
+        either = [(slot_of(linear + two), slot_of(linear + three)) for two, three in EITHER]
+        two = is_two(r)
+        picks = fixed + [jnp.where(two == 1, p, q) for p, q in either]
+        weight = two.astype(f32)
+
+        def add(acc, k, part):
+            if k < len(FIXED):
+                acc[fixed[k]] += part
+            else:
+                p, q = either[k - len(FIXED)]
+                acc[p] += part * weight
+                acc[q] += part * (1.0 - weight)
+
+        return picks, add
 
     def heads_of(array, r):
         return jnp.concatenate([array[r, :, h * HD : (h + 1) * HD] for h in range(PER)], 0)
 
-    def scores(r, _):
+    def folded(array):
+        return array.reshape(BLOCK // 8, 8, WIDE)
+
+    def scores(r):
         q = heads_of(q_all, r)
-        picks = listed_slots(*slots(r), is_two(r))
+        picks, _ = slots(r)
         high = None
-        for k, slot in enumerate(picks):
-            s = dot(kw[slot], q, 1, 1)
+        for k in range(LISTED):
+            s = dot(kw[picks[k]], q, 1, 1)
             s_all[r, k] = s
-            top = s.reshape(16, 8, WIDE).max(0)
+            top = folded(s).max(0)
             high = top if high is None else jnp.maximum(high, top)
-        high_all[r] = high
+        high = high.max(0, keepdims=True)
+        total = jnp.zeros((8, WIDE), f32)
+        for k in range(LISTED):
+            total = total + folded(jnp.exp2((s_all[r, k] - high) * scale_two)).sum(0)
+        log_total = jnp.log(total.sum(0, keepdims=True)) * LOG2E
+        for k in range(LISTED):
+            s_all[r, k] = (s_all[r, k] - high) * scale_two - log_total
+        shift_all[r] = jnp.broadcast_to(high + log_total / scale_two, (8, WIDE))
+
+    def even_scores(i, _):
+        @pl.when(i == 1)
+        def _():
+            received(q_odd)
+            start(g_x)
+
+        @pl.when(i == 2)
+        def _():
+            received(v_own[:1])
+            start(v_other)
+
+        scores(i * OWN)
         return 0
 
-    for copy in here_q:
-        copy.wait()
-    received(q_x)
-    received(k_own[1:])
-    received(k_other)
-    lax.fori_loop(0, ROWS // 2, scores, 0)
-    received(v_own[:1])
-    start(v_other)
-    lax.fori_loop(ROWS // 2, ROWS, scores, 0)
-    for copy in here_g:
-        copy.wait()
+    def odd_scores(i, _):
+        scores(i * OWN + 1)
+        return 0
+
+    lax.fori_loop(0, NX, even_scores, 0)
+    lax.fori_loop(0, NX, odd_scores, 0)
+    wait(here_g)
     received(g_x)
     received(v_own[1:])
     received(v_other)
@@ -216,7 +251,10 @@
             return pltpu.make_async_copy(od.at[r, which], dst, od_recv.at[n])
         return remote(od.at[r, which], dst, od_send.at[n], od_recv.at[n], at(0, NX - d, 0))
 
-    def send_back(r, which, out):
+    def send_back(r, which, out, result):
+        for h in range(PER):
+            od[r, which, :, h * HD : (h + 1) * HD] = result[h * BLOCK : (h + 1) * BLOCK].astype(bf16)
+
         @pl.when(r < OWN)
         def _():
             back(r, which, out, True).start()
@@ -225,90 +263,125 @@
         def _():
             back(r, which, out, False).start()
 
-    def row(step, _):
+    def outputs(step, _):
         r = lax.rem(step + OWN, ROWS)
-        q = heads_of(q_all, r)
         g = heads_of(g_all, r)
-        fixed, either = slots(r)
-        two = is_two(r)
-        picks = listed_slots(fixed, either, two)
-        weight = two.astype(f32)
-
-        def add(acc, k, part):
-            if k < len(FIXED):
-                acc[fixed[k]] += part
-            else:
-                p, q = either[k - len(FIXED)]
-                acc[p] += part * weight
-                acc[q] += part * (1.0 - weight)
-
-        high = high_all[r].max(0, keepdims=True)
-        total = jnp.zeros((8, WIDE), f32)
-        for k in range(LISTED):
-            e = jnp.exp((s_all[r, k] - high) * scale)
-            e_scr[k] = e
-            total = total + e.reshape(16, 8, WIDE).sum(0)
-        inverse = 1.0 / total.sum(0, keepdims=True)
+        picks, add = slots(r)
         o = None
         for k in range(LISTED):
-            p = (e_scr[k] * inverse).astype(bf16)
+            p = jnp.exp2(s_all[r, k]).astype(bf16)
             add(dv_acc, k, dot(p, g, 1, 0))
             part = dot(p, vw[picks[k]], 0, 0)
             o = part if o is None else o + part
-        for h in range(PER):
-            od[r, 0, :, h * HD : (h + 1) * HD] = o[h * BLOCK : (h + 1) * BLOCK].astype(bf16)
-        send_back(r, 0, attended)
+        send_back(r, 0, attended, o)
         row_dot = (g.astype(f32) * o).sum(-1, keepdims=True)
-        row_dot = jnp.broadcast_to(row_dot, (WIDE, HD)).T[0:1]
-        tau = jnp.zeros((8, WIDE), f32)
-        dq = None
-        factor = inverse * scale
-        for k in range(LISTED):
-            t = e_scr[k] * (dot(vw[picks[k]], g, 1, 1) - row_dot)
-            tau = tau + (t * s_all[r, k]).reshape(16, 8, WIDE).sum(0)
-            ds = (t * factor).astype(bf16)
-            add(dk_acc, k, dot(ds, q, 1, 0))
-            part = dot(ds, kw[picks[k]], 0, 0)
-            dq = part if dq is None else dq + part
-        for h in range(PER):
-            od[r, 1, :, h * HD : (h + 1) * HD] = dq[h * BLOCK : (h + 1) * BLOCK].astype(bf16)
-        send_back(r, 1, query_grad)
-        tau_acc[...] += tau * inverse
+        dot_all[r] = jnp.broadcast_to(row_dot, (WIDE, HD)).T[0:8]
         return 0
 
-    lax.fori_loop(0, ROWS, row, 0)
+    lax.fori_loop(0, ROWS, outputs, 0)
 
     accs = (dv_acc, dk_acc)
-    y_out = []
-    for kv in range(2):
+    outs = (value_grad, key_grad)
+
+    def y_copy(kv, half, side):
+        n = kv * 4 + half * 2 + side
+        return remote(stage.at[n], arrived.at[n], out_send.at[n], out_recv.at[n], at(3 if side == 0 else 1, 0, 0))
+
+    def y_pair(kv, half):
+        return [y_copy(kv, half, side) for side in range(2)]
+
+    def z_copy(kv):
+        return remote(z_stage.at[kv], z_arrived.at[kv], out_send.at[8 + kv], out_recv.at[8 + kv], at(0, 0, 1))
+
+    def x_copies(kv, local):
+        copies = []
+        for d in range(NX):
+            from_x = lax.rem(x - d + NX, NX)
+            for m in range(OWN):
+                src = final.at[kv, from_x * OWN + m]
+                dst = columns(outs[kv], m, x, HD)
+                n = 10 + (kv * NX + d) * OWN + m
+                if local and d == 0:
+                    copies.append(pltpu.make_async_copy(src, dst, out_recv.at[n]))
+                if not local and d > 0:
+                    copies.append(remote(src, dst, out_send.at[n], out_recv.at[n], at(0, NX - d, 0)))
+        return copies
+
+    def to_y(kv):
         for half in range(2):
             for side in range(2):
-                n = kv * 4 + half * 2 + side
                 begin = side * 2 * PLANE + (1 - z if half == 0 else z) * HALF
-                stage[n] = accs[kv][pl.ds(begin, HALF)].astype(bf16)
-                copy = remote(stage.at[n], arrived.at[n], out_send.at[n], out_recv.at[n], at(3 if side == 0 else 1, 0, 0))
-                copy.start()
-                y_out.append(copy)
-
-    tau_waits = []
+                stage[kv * 4 + half * 2 + side] = accs[kv][pl.ds(begin, HALF)].astype(bf16)
+                y_copy(kv, half, side).start()
+
+    def to_z(kv):
+        received(y_pair(kv, 0))
+        summed = accs[kv][pl.ds(other_half, HALF)] + arrived[kv * 4].astype(f32) + arrived[kv * 4 + 1].astype(f32)
+        z_stage[kv] = summed.astype(bf16)
+        z_copy(kv).start()
+
+    def to_x(kv):
+        received(y_pair(kv, 1))
+        summed = accs[kv][pl.ds(near_half, HALF)] + arrived[kv * 4 + 2].astype(f32) + arrived[kv * 4 + 3].astype(f32)
+        z_copy(kv).wait_recv()
+        final[kv] = (summed + z_arrived[kv].astype(f32)).astype(bf16)
+        start(x_copies(kv, False))
+        start(x_copies(kv, True))
+
+    to_y(0)
+    tau_acc[...] = jnp.zeros_like(tau_acc)
+
+    def score_grads(step, _):
+        @pl.when(step == 4)
+        def _():
+            to_z(0)
+
+        @pl.when(step == 7)
+        def _():
+            to_x(0)
+
+        r = step
+        q = heads_of(q_all, r)
+        g = heads_of(g_all, r)
+        picks, add = slots(r)
+        row_dot = dot_all[r][0:1]
+        first = jnp.zeros((8, WIDE), f32)
+        second = jnp.zeros((8, WIDE), f32)
+        for k in range(LISTED):
+            s = s_all[r, k]
+            t = jnp.exp2(s) * (dot(vw[picks[k]], g, 1, 1) - row_dot)
+            first = first + folded(t * s).sum(0)
+            second = second + folded(t).sum(0)
+            ds = (t * scale).astype(bf16)
+            ds_all[r, k] = ds
+            add(dk_acc, k, dot(ds, q, 1, 0))
+        tau_acc[...] += first / scale_two + second * shift_all[r]
+        return 0
+
+    lax.fori_loop(0, ROWS, score_grads, 0)
+    to_y(1)
+
     parts = jnp.concatenate([tau_acc[:, h * BLOCK : (h + 1) * BLOCK].sum(0, keepdims=True) for h in range(PER)], 0)
     tau_x[x] = jnp.concatenate([parts, jnp.zeros_like(parts)], 0)
     tau_first = [remote(tau_x.at[x], tau_x.at[x], tau_send.at[d - 1], tau_recv.at[d - 1], at(0, d, 0)) for d in (1, 2, 3)]
     start(tau_first)
+
+    def query_grads(step, _):
+        r = lax.rem(step + OWN, ROWS)
+        picks, _ = slots(r)
+        dq = None
+        for k in range(LISTED):
+            part = dot(ds_all[r, k], kw[picks[k]], 0, 0)
+            dq = part if dq is None else dq + part
+        send_back(r, 1, query_grad, dq)
+        return 0
+
+    lax.fori_loop(0, ROWS, query_grads, 0)
+    to_z(1)
     received(tau_first)
     tau_y[y] = tau_x[...]
     tau_second = [remote(tau_y.at[y], tau_y.at[y], tau_send.at[d + 2], tau_recv.at[d + 2], at(d, 0, 0)) for d in (1, 2, 3)]
     start(tau_second)
-
-    z_out = []
-    for kv in range(2):
-        received(y_out[kv * 4 : kv * 4 + 2])
-        summed = accs[kv][pl.ds(other_half, HALF)] + arrived[kv * 4].astype(f32) + arrived[kv * 4 + 1].astype(f32)
-        z_stage[kv] = summed.astype(bf16)
-        copy = remote(z_stage.at[kv], z_arrived.at[kv], out_send.at[8 + kv], out_recv.at[8 + kv], at(0, 0, 1))
-        copy.start()
-        z_out.append(copy)
-
     received(tau_second)
     spot = z * BATCH + batch
     tau_z[spot] = tau_y[0] + tau_y[1] + tau_y[2] + tau_y[3]
@@ -319,28 +392,7 @@
                 n = 6 + len(tau_third)
                 tau_third.append(remote(tau_z.at[spot], tau_z.at[spot], tau_send.at[n], tau_recv.at[n], far(dz, db)))
     start(tau_third)
-
-    x_out = []
-    x_local = []
-    for kv, out in enumerate((value_grad, key_grad)):
-        received(y_out[kv * 4 + 2 : kv * 4 + 4])
-        received(z_out[kv : kv + 1])
-        summed = accs[kv][pl.ds(near_half, HALF)] + arrived[kv * 4 + 2].astype(f32) + arrived[kv * 4 + 3].astype(f32)
-        final[kv] = (summed + z_arrived[kv].astype(f32)).astype(bf16)
-        for d in range(NX):
-            from_x = lax.rem(x - d + NX, NX)
-            for m in range(OWN):
-                src = final.at[kv, from_x * OWN + m]
-                dst = columns(out, m, x, HD)
-                n = 10 + (kv * NX + d) * OWN + m
-                if d == 0:
-                    copy = pltpu.make_async_copy(src, dst, out_recv.at[n])
-                    x_local.append(copy)
-                else:
-                    copy = remote(src, dst, out_send.at[n], out_recv.at[n], at(0, NX - d, 0))
-                    x_out.append(copy)
-                copy.start()
-
+    to_x(1)
     received(tau_third)
     whole = tau_z[0]
     for n in range(1, NZ * BATCH):
@@ -350,16 +402,27 @@
         for h in range(PER):
             tau_out[n * PER + h] = jnp.sum(whole[n, h : h + 1, :]) / norm
 
-    received(x_out)
-    for copy in x_local:
-        copy.wait()
     for which, out in enumerate((attended, query_grad)):
         for r in range(ROWS):
             back(r, which, out, r < OWN).wait()
-    for copy in k_x + v_x + q_x + g_x + k_own + k_other + v_own + v_other:
+    for kv in range(2):
+        received(x_copies(kv, False))
+        wait(x_copies(kv, True))
+    sent = k_x + v_x + q_x + g_x + k_own + k_other + v_own + v_other + tau_first + tau_second + tau_third
+    for kv in range(2):
+        sent += y_pair(kv, 0) + y_pair(kv, 1) + [z_copy(kv)] + x_copies(kv, False)
+    for copy in sent:
         copy.wait_send()
-    for copy in y_out + z_out + x_out + tau_first + tau_second + tau_third:
-        copy.wait_send()
+
+
+def copy_out(*refs):
+    n = len(refs) // 2
+    sems = refs[-1]
+    copies = [pltpu.make_async_copy(refs[i], refs[n + i], sems.at[i]) for i in range(n)]
+    for copy in copies:
+        copy.start()
+    for copy in copies:
+        copy.wait()
 
 
 def body(queries, keys, values, tau, out_grad, key_blocks):
@@ -386,8 +449,9 @@
             pltpu.VMEM((ROWS, BLOCK, WIDE), bf16),
             pltpu.VMEM((ROWS, BLOCK, WIDE), bf16),
             pltpu.VMEM((ROWS, LISTED, BLOCK, WIDE), f32),
+            pltpu.VMEM((ROWS, LISTED, BLOCK, WIDE), bf16),
             pltpu.VMEM((ROWS, 8, WIDE), f32),
-            pltpu.VMEM((LISTED, BLOCK, WIDE), f32),
+            pltpu.VMEM((ROWS, 8, WIDE), f32),
             pltpu.VMEM((WINDOW, BLOCK, HD), f32),
             pltpu.VMEM((WINDOW, BLOCK, HD), f32),
             pltpu.VMEM((ROWS, 2, BLOCK, WIDE), bf16),
@@ -413,7 +477,15 @@
         compiler_params=pltpu.CompilerParams(
             collective_id=0, has_side_effects=True, vmem_limit_bytes=62 << 20
         ),
-    )(key_blocks, tau, *blocked)
+    )(key_blocks.transpose(2, 0, 1), tau, *blocked)
+    outs = pl.pallas_call(
+        copy_out,
+        name="copy_out",
+        out_shape=tuple(jax.ShapeDtypeStruct(o.shape, o.dtype) for o in outs),
+        in_specs=[anywhere] * len(outs),
+        out_specs=(anywhere,) * len(outs),
+        scratch_shapes=[pltpu.SemaphoreType.DMA((len(outs),))],
+    )(*outs)
     return tuple(o.reshape(a.shape) for o, a in zip(outs[:4], (queries, queries, keys, keys))) + (outs[4],)
 
 

time: 121 us -> 180 us (1.49)
  Pallas kernels: 113 us -> 179 us
  local copies, waits for them, and re-layouts: 7.26 us -> 0 us
    pallas_call x0 -> x1, Pallas kernels: none -> 80.6 us  [body(): pl.pallas_call(copy_out, name='copy_out', out_shape=tuple((jax.ShapeDtype...]
    pallas_call x1, Pallas kernels: 113 us -> 98.3 us  [body(): pl.pallas_call(kernel, name='attention', out_shape=(jax.ShapeDtypeStruct(...]
    unnamed x14 -> x0, local copies, waits for them, and re-layouts: 7.26 us -> none
where the time goes in v3:
time: 180 us
  Pallas kernels  179 us (99%)
    pallas_call x1, Pallas kernels, body(): pl.pallas_call(kernel, name='attention', out_shape=(jax.ShapeDtypeStruct(...  98.3 us
    pallas_call x1, Pallas kernels, body(): pl.pallas_call(copy_out, name='copy_out', out_shape=tuple((jax.ShapeDtype...  80.6 us

profile of v3, /device:TPU:0, one launch (start us, length us, event | category | flops | bytes accessed | tf_op | source)
XLA Modules:
  0.0 179.6 jit_solution(10368309382631239250)
XLA Ops:
  0.6 98.3 %attention.1 = (bf16[2,128,2048]{2,1,0:T(8,128)(2,1)}, bf16[2,128,2048]{2,1,0:T(8,128)(2,1)}, bf16[2,128,512]{2,1,0:T(8,128)(2,1)}, bf16[2,128,512]{2,1,0:T(8,128)(2,1)}, f32[16]{0:T(128)}) custom-call(s32[13,4,64]{2,1,0:T(4,128)} %bitcast.13, f32[16]{0:T(128)} %tau_ref.1, bf16[2,128,2048]{2,1,0:T(8,128)(2,1)} %bitcast.9, bf16[2,128,512]{2,1,0:T(8,128)(2,1)} %bitcast.11, ...), custom_call_target="tpu_custom_call" | custom-call | tf_op jit(solution)/shard_map/attention/pallas_call | solution.py:434
  99.0 80.6 %copy_out.1 = (bf16[2,128,2048]{2,1,0:T(8,128)(2,1)}, bf16[2,128,2048]{2,1,0:T(8,128)(2,1)}, bf16[2,128,512]{2,1,0:T(8,128)(2,1)}, bf16[2,128,512]{2,1,0:T(8,128)(2,1)}, f32[16]{0:T(128)}) custom-call(bf16[2,128,2048]{2,1,0:T(8,128)(2,1)} %get-tuple-element.15.refs_0_, bf16[2,128,2048]{2,1,0:T(8,128)(2,1)} %get-tuple-element.16.refs_1_, ...), custom_call_target="tpu_custom_call" | custom-call | tf_op jit(solution)/shard_map/copy_out/pallas_call | solution.py:481

commit v4 on v3

--- a/solution.py
+++ b/solution.py
@@ -20,6 +20,8 @@
 HALF = NX * OWN
 PLANE = NZ * HALF
 WINDOW = 3 * PLANE
+PARTS = 2
+CHUNK = HALF // PARTS
 TOKENS = OWN * BLOCK
 FIXED = (-1, 0, 1, 6, -6)
 EITHER = ((2, 3), (-2, -3), (4, 9), (-4, -9), (8, 12), (-8, -12), (10, 15), (-10, -15))
@@ -44,7 +46,7 @@
     attended, query_grad, key_grad, value_grad, tau_out,
     kw, vw, q_all, g_all, s_all, ds_all, shift_all, dot_all, dk_acc, dv_acc, od,
     stage, arrived, z_stage, z_arrived, final, tau_acc, tau_x, tau_y, tau_z,
-    here_sem, in_send, in_recv, od_send, od_recv, out_send, out_recv, tau_send, tau_recv,
+    here_sem, in_send, in_recv, od_send, od_recv, y_send, y_recv, z_send, z_recv, x_send, x_recv, tau_send, tau_recv,
 ):
     me = lax.axis_index("ctx")
     batch = lax.axis_index("batch")
@@ -147,19 +149,21 @@
     wait(here_k)
     received(k_x)
     start(k_own)
+    start(v_x)
     start(q_even)
-    start(v_x)
+    wait(here_v)
+    received(v_x)
+    start(v_own)
+    start(q_odd)
+    start(g_x)
     received(k_own[:1])
     start(k_other)
-    wait(here_v)
+    received(v_own[:1])
+    start(v_other)
+    wait(here_q)
     received(q_even)
-    received(v_x)
-    start(v_own[:1])
-    start(q_odd)
-    wait(here_q)
     received(k_own[1:])
     received(k_other)
-    start(v_own[1:])
 
     def row_place(r):
         return lax.rem(x - r // OWN + NX, NX) * (NZ * OWN) + z * OWN + lax.rem(r, OWN)
@@ -205,30 +209,18 @@
         picks, _ = slots(r)
         high = None
         for k in range(LISTED):
-            s = dot(kw[picks[k]], q, 1, 1)
+            s = dot(kw[picks[k]], q, 1, 1) * scale_two
             s_all[r, k] = s
             top = folded(s).max(0)
             high = top if high is None else jnp.maximum(high, top)
         high = high.max(0, keepdims=True)
         total = jnp.zeros((8, WIDE), f32)
         for k in range(LISTED):
-            total = total + folded(jnp.exp2((s_all[r, k] - high) * scale_two)).sum(0)
+            total = total + folded(jnp.exp2(s_all[r, k] - high)).sum(0)
         log_total = jnp.log(total.sum(0, keepdims=True)) * LOG2E
-        for k in range(LISTED):
-            s_all[r, k] = (s_all[r, k] - high) * scale_two - log_total
-        shift_all[r] = jnp.broadcast_to(high + log_total / scale_two, (8, WIDE))
+        shift_all[r] = jnp.broadcast_to(high + log_total, (8, WIDE))
 
     def even_scores(i, _):
-        @pl.when(i == 1)
-        def _():
-            received(q_odd)
-            start(g_x)
-
-        @pl.when(i == 2)
-        def _():
-            received(v_own[:1])
-            start(v_other)
-
         scores(i * OWN)
         return 0
 
@@ -237,6 +229,7 @@
         return 0
 
     lax.fori_loop(0, NX, even_scores, 0)
+    received(q_odd)
     lax.fori_loop(0, NX, odd_scores, 0)
     wait(here_g)
     received(g_x)
@@ -267,9 +260,10 @@
         r = lax.rem(step + OWN, ROWS)
         g = heads_of(g_all, r)
         picks, add = slots(r)
+        shift = shift_all[r, 0:1]
         o = None
         for k in range(LISTED):
-            p = jnp.exp2(s_all[r, k]).astype(bf16)
+            p = jnp.exp2(s_all[r, k] - shift).astype(bf16)
             add(dv_acc, k, dot(p, g, 1, 0))
             part = dot(p, vw[picks[k]], 0, 0)
             o = part if o is None else o + part
@@ -283,79 +277,90 @@
     accs = (dv_acc, dk_acc)
     outs = (value_grad, key_grad)
 
-    def y_copy(kv, half, side):
-        n = kv * 4 + half * 2 + side
-        return remote(stage.at[n], arrived.at[n], out_send.at[n], out_recv.at[n], at(3 if side == 0 else 1, 0, 0))
-
-    def y_pair(kv, half):
-        return [y_copy(kv, half, side) for side in range(2)]
-
-    def z_copy(kv):
-        return remote(z_stage.at[kv], z_arrived.at[kv], out_send.at[8 + kv], out_recv.at[8 + kv], at(0, 0, 1))
-
-    def x_copies(kv, local):
-        copies = []
-        for d in range(NX):
-            from_x = lax.rem(x - d + NX, NX)
-            for m in range(OWN):
-                src = final.at[kv, from_x * OWN + m]
-                dst = columns(outs[kv], m, x, HD)
-                n = 10 + (kv * NX + d) * OWN + m
-                if local and d == 0:
-                    copies.append(pltpu.make_async_copy(src, dst, out_recv.at[n]))
-                if not local and d > 0:
-                    copies.append(remote(src, dst, out_send.at[n], out_recv.at[n], at(0, NX - d, 0)))
-        return copies
+    def y_copy(kv, half, part, side):
+        n = ((kv * 2 + half) * PARTS + part) * 2 + side
+        return remote(stage.at[n], arrived.at[n], y_send.at[n], y_recv.at[n], at(3 if side == 0 else 1, 0, 0))
+
+    def z_copy(kv, part):
+        n = kv * PARTS + part
+        return remote(z_stage.at[n], z_arrived.at[n], z_send.at[n], z_recv.at[n], at(0, 0, 1))
+
+    def x_copy(kv, to, m, local):
+        src = final.at[kv, to * OWN + m]
+        dst = columns(outs[kv], m, x, HD)
+        n = (kv * NX + x) * OWN + m
+        if local:
+            return pltpu.make_async_copy(src, dst, x_recv.at[n])
+        return remote(src, dst, x_send.at[(kv * NX + to) * OWN + m], x_recv.at[n], {"ctx": index_of(y, to, z)})
+
+    def x_arrival(kv, d, m):
+        dst = columns(outs[kv], m, lax.rem(x + d, NX), HD)
+        n = (kv * NX + lax.rem(x + d, NX)) * OWN + m
+        return remote(final.at[kv, m], dst, x_send.at[n], x_recv.at[n], at(0, d, 0))
+
+    def both(kv, half, part):
+        return [y_copy(kv, half, part, side) for side in range(2)]
 
     def to_y(kv):
         for half in range(2):
-            for side in range(2):
-                begin = side * 2 * PLANE + (1 - z if half == 0 else z) * HALF
-                stage[kv * 4 + half * 2 + side] = accs[kv][pl.ds(begin, HALF)].astype(bf16)
-                y_copy(kv, half, side).start()
-
-    def to_z(kv):
-        received(y_pair(kv, 0))
-        summed = accs[kv][pl.ds(other_half, HALF)] + arrived[kv * 4].astype(f32) + arrived[kv * 4 + 1].astype(f32)
-        z_stage[kv] = summed.astype(bf16)
-        z_copy(kv).start()
-
-    def to_x(kv):
-        received(y_pair(kv, 1))
-        summed = accs[kv][pl.ds(near_half, HALF)] + arrived[kv * 4 + 2].astype(f32) + arrived[kv * 4 + 3].astype(f32)
-        z_copy(kv).wait_recv()
-        final[kv] = (summed + z_arrived[kv].astype(f32)).astype(bf16)
-        start(x_copies(kv, False))
-        start(x_copies(kv, True))
+            for part in range(PARTS):
+                for side in range(2):
+                    begin = side * 2 * PLANE + (1 - z if half == 0 else z) * HALF + part * CHUNK
+                    stage[((kv * 2 + half) * PARTS + part) * 2 + side] = accs[kv][pl.ds(begin, CHUNK)].astype(bf16)
+                    y_copy(kv, half, part, side).start()
+
+    def collected(kv, half, part, begin):
+        received(both(kv, half, part))
+        n = ((kv * 2 + half) * PARTS + part) * 2
+        summed = accs[kv][pl.ds(begin + part * CHUNK, CHUNK)]
+        return summed + arrived[n].astype(f32) + arrived[n + 1].astype(f32)
+
+    def to_z(kv, part):
+        z_stage[kv * PARTS + part] = collected(kv, 0, part, other_half).astype(bf16)
+        z_copy(kv, part).start()
+
+    def to_x(kv, part):
+        summed = collected(kv, 1, part, near_half)
+        z_copy(kv, part).wait_recv()
+        summed = summed + z_arrived[kv * PARTS + part].astype(f32)
+        final[kv, part * CHUNK : (part + 1) * CHUNK] = summed.astype(bf16)
+        for i in range(CHUNK // OWN):
+            to = part * (CHUNK // OWN) + i
+
+            @pl.when(to == x)
+            def _():
+                for m in range(OWN):
+                    x_copy(kv, to, m, True).start()
+
+            @pl.when(to != x)
+            def _():
+                for m in range(OWN):
+                    x_copy(kv, to, m, False).start()
 
     to_y(0)
     tau_acc[...] = jnp.zeros_like(tau_acc)
 
     def score_grads(step, _):
-        @pl.when(step == 4)
+        @pl.when(step == 5)
         def _():
-            to_z(0)
-
-        @pl.when(step == 7)
-        def _():
-            to_x(0)
+            for part in range(PARTS):
+                to_z(0, part)
 
         r = step
         q = heads_of(q_all, r)
         g = heads_of(g_all, r)
         picks, add = slots(r)
-        row_dot = dot_all[r][0:1]
-        first = jnp.zeros((8, WIDE), f32)
-        second = jnp.zeros((8, WIDE), f32)
+        row_dot = dot_all[r, 0:1]
+        shift = shift_all[r, 0:1]
+        tau = jnp.zeros((8, WIDE), f32)
         for k in range(LISTED):
             s = s_all[r, k]
-            t = jnp.exp2(s) * (dot(vw[picks[k]], g, 1, 1) - row_dot)
-            first = first + folded(t * s).sum(0)
-            second = second + folded(t).sum(0)
-            ds = (t * scale).astype(bf16)
-            ds_all[r, k] = ds
-            add(dk_acc, k, dot(ds, q, 1, 0))
-        tau_acc[...] += first / scale_two + second * shift_all[r]
+            t = jnp.exp2(s - shift) * (dot(vw[picks[k]], g, 1, 1) - row_dot)
+            tau = tau + folded(t * s).sum(0)
+            ds_all[r, k] = (t * scale).astype(bf16)
+        for k in range(LISTED):
+            add(dk_acc, k, dot(ds_all[r, k], q, 1, 0))
+        tau_acc[...] += tau / scale_two
         return 0
 
     lax.fori_loop(0, ROWS, score_grads, 0)
@@ -376,8 +381,13 @@
         send_back(r, 1, query_grad, dq)
         return 0
 
-    lax.fori_loop(0, ROWS, query_grads, 0)
-    to_z(1)
+    lax.fori_loop(0, ROWS // 2, query_grads, 0)
+    to_z(1, 0)
+    lax.fori_loop(ROWS // 2, ROWS, query_grads, 0)
+    for part in range(1, PARTS):
+        to_z(1, part)
+    for part in range(PARTS):
+        to_x(0, part)
     received(tau_first)
     tau_y[y] = tau_x[...]
     tau_second = [remote(tau_y.at[y], tau_y.at[y], tau_send.at[d + 2], tau_recv.at[d + 2], at(d, 0, 0)) for d in (1, 2, 3)]
@@ -392,7 +402,8 @@
                 n = 6 + len(tau_third)
                 tau_third.append(remote(tau_z.at[spot], tau_z.at[spot], tau_send.at[n], tau_recv.at[n], far(dz, db)))
     start(tau_third)
-    to_x(1)
+    for part in range(PARTS):
+        to_x(1, part)
     received(tau_third)
     whole = tau_z[0]
     for n in range(1, NZ * BATCH):
@@ -406,22 +417,37 @@
         for r in range(ROWS):
             back(r, which, out, r < OWN).wait()
     for kv in range(2):
-        received(x_copies(kv, False))
-        wait(x_copies(kv, True))
-    sent = k_x + v_x + q_x + g_x + k_own + k_other + v_own + v_other + tau_first + tau_second + tau_third
-    for kv in range(2):
-        sent += y_pair(kv, 0) + y_pair(kv, 1) + [z_copy(kv)] + x_copies(kv, False)
-    for copy in sent:
+        for m in range(OWN):
+            x_copy(kv, x, m, True).wait()
+            for d in (1, 2, 3):
+                x_arrival(kv, d, m).wait_recv()
+                x_copy(kv, lax.rem(x + d, NX), m, False).wait_send()
+        for part in range(PARTS):
+            z_copy(kv, part).wait_send()
+            for half in range(2):
+                for copy in both(kv, half, part):
+                    copy.wait_send()
+    for copy in k_x + v_x + q_x + g_x + k_own + k_other + v_own + v_other + tau_first + tau_second + tau_third:
         copy.wait_send()
 
 
 def copy_out(*refs):
-    n = len(refs) // 2
-    sems = refs[-1]
-    copies = [pltpu.make_async_copy(refs[i], refs[n + i], sems.at[i]) for i in range(n)]
-    for copy in copies:
+    n = (len(refs) - 2) // 3
+    sources, results, held = refs[:n], refs[n : 2 * n], refs[2 * n : 3 * n]
+    in_sem, out_sem = refs[3 * n :]
+    pieces = [(i, m) for i in range(n) for m in range(OWN if i < n - 1 else 1)]
+
+    def piece(ref, i, m):
+        return ref.at[m] if i < n - 1 else ref
+
+    into = [pltpu.make_async_copy(piece(sources[i], i, m), piece(held[i], i, m), in_sem.at[j]) for j, (i, m) in enumerate(pieces)]
+    away = [pltpu.make_async_copy(piece(held[i], i, m), piece(results[i], i, m), out_sem.at[j]) for j, (i, m) in enumerate(pieces)]
+    for copy in into:
         copy.start()
-    for copy in copies:
+    for first, second in zip(into, away):
+        first.wait()
+        second.start()
+    for copy in away:
         copy.wait()
 
 
@@ -429,7 +455,7 @@
     anywhere = pl.BlockSpec(memory_space=pl.ANY)
     scalars = pl.BlockSpec(memory_space=pltpu.SMEM)
     shape = lambda a: (OWN, BLOCK, a.shape[2])
-    half = (HALF, BLOCK, HD)
+    chunk = (CHUNK, BLOCK, HD)
     blocked = [a.reshape(shape(a)) for a in (queries, keys, values, out_grad)]
     outs = pl.pallas_call(
         kernel,
@@ -455,11 +481,11 @@
             pltpu.VMEM((WINDOW, BLOCK, HD), f32),
             pltpu.VMEM((WINDOW, BLOCK, HD), f32),
             pltpu.VMEM((ROWS, 2, BLOCK, WIDE), bf16),
-            pltpu.VMEM((8,) + half, bf16),
-            pltpu.VMEM((8,) + half, bf16),
-            pltpu.VMEM((2,) + half, bf16),
-            pltpu.VMEM((2,) + half, bf16),
-            pltpu.VMEM((2,) + half, bf16),
+            pltpu.VMEM((8 * PARTS,) + chunk, bf16),
+            pltpu.VMEM((8 * PARTS,) + chunk, bf16),
+            pltpu.VMEM((2 * PARTS,) + chunk, bf16),
+            pltpu.VMEM((2 * PARTS,) + chunk, bf16),
+            pltpu.VMEM((2, HALF, BLOCK, HD), bf16),
             pltpu.VMEM((8, WIDE), f32),
             pltpu.VMEM((NX, 8, BLOCK), f32),
             pltpu.VMEM((NY, NX, 8, BLOCK), f32),
@@ -469,8 +495,12 @@
             pltpu.SemaphoreType.DMA((34,)),
             pltpu.SemaphoreType.DMA((2 * ROWS,)),
             pltpu.SemaphoreType.DMA((2 * ROWS,)),
-            pltpu.SemaphoreType.DMA((26,)),
-            pltpu.SemaphoreType.DMA((26,)),
+            pltpu.SemaphoreType.DMA((8 * PARTS,)),
+            pltpu.SemaphoreType.DMA((8 * PARTS,)),
+            pltpu.SemaphoreType.DMA((2 * PARTS,)),
+            pltpu.SemaphoreType.DMA((2 * PARTS,)),
+            pltpu.SemaphoreType.DMA((2 * NX * OWN,)),
+            pltpu.SemaphoreType.DMA((2 * NX * OWN,)),
             pltpu.SemaphoreType.DMA((13,)),
             pltpu.SemaphoreType.DMA((13,)),
         ],
@@ -484,7 +514,7 @@
         out_shape=tuple(jax.ShapeDtypeStruct(o.shape, o.dtype) for o in outs),
         in_specs=[anywhere] * len(outs),
         out_specs=(anywhere,) * len(outs),
-        scratch_shapes=[pltpu.SemaphoreType.DMA((len(outs),))],
+        scratch_shapes=[pltpu.VMEM(o.shape, o.dtype) for o in outs] + [pltpu.SemaphoreType.DMA((9,))] * 2,
     )(*outs)
     return tuple(o.reshape(a.shape) for o, a in zip(outs[:4], (queries, queries, keys, keys))) + (outs[4],)
 

time: 180 us -> 90.4 us (0.50)
  Pallas kernels: 179 us -> 89.4 us
    pallas_call x1, Pallas kernels: 80.6 us -> 2.68 us  [body(): pl.pallas_call(copy_out, name='copy_out', out_shape=tuple((jax.ShapeDtype...]
    pallas_call x1, Pallas kernels: 98.3 us -> 86.8 us  [body(): pl.pallas_call(kernel, name='attention', out_shape=(jax.ShapeDtypeStruct(...]
where the time goes in v4:
time: 90.4 us; the launch traced here: 90.1 us
  Pallas kernels  89.4 us (99%)
    pallas_call x1, Pallas kernels, body(): pl.pallas_call(kernel, name='attention', out_shape=(jax.ShapeDtypeStruct(...  86.8 us
    pallas_call x1, Pallas kernels, body(): pl.pallas_call(copy_out, name='copy_out', out_shape=tuple((jax.ShapeDtype...  2.68 us

profile of v4, /device:TPU:0, one launch (start us, length us, event | category | flops | bytes accessed | tf_op | source)
XLA Modules:
  0.0 90.1 jit_solution(12306293596363105432)
XLA Ops:
  0.6 86.8 %attention.1 = (bf16[2,128,2048]{2,1,0:T(8,128)(2,1)}, bf16[2,128,2048]{2,1,0:T(8,128)(2,1)}, bf16[2,128,512]{2,1,0:T(8,128)(2,1)}, bf16[2,128,512]{2,1,0:T(8,128)(2,1)}, f32[16]{0:T(128)}) custom-call(s32[13,4,64]{2,1,0:T(4,128)} %bitcast.13, f32[16]{0:T(128)} %tau_ref.1, bf16[2,128,2048]{2,1,0:T(8,128)(2,1)} %bitcast.9, bf16[2,128,512]{2,1,0:T(8,128)(2,1)} %bitcast.11, ...), custom_call_target="tpu_custom_call" | custom-call | tf_op jit(solution)/shard_map/attention/pallas_call | solution.py:460
  87.4 2.7 %copy_out.1 = (bf16[2,128,2048]{2,1,0:T(8,128)(2,1)}, bf16[2,128,2048]{2,1,0:T(8,128)(2,1)}, bf16[2,128,512]{2,1,0:T(8,128)(2,1)}, bf16[2,128,512]{2,1,0:T(8,128)(2,1)}, f32[16]{0:T(128)}) custom-call(bf16[2,128,2048]{2,1,0:T(8,128)(2,1)} %get-tuple-element.15.refs_0_, bf16[2,128,2048]{2,1,0:T(8,128)(2,1)} %get-tuple-element.16.refs_1_, ...), custom_call_target="tpu_custom_call" | custom-call | tf_op jit(solution)/shard_map/copy_out/pallas_call | solution.py:511

commit v5 on v4

--- a/solution.py
+++ b/solution.py
@@ -111,20 +111,35 @@
     q_x = along_x(queries, WIDE, lambda d, n: q_all.at[d * OWN + n], 12)
     g_x = along_x(grads, WIDE, lambda d, n: g_all.at[d * OWN + n], 18)
 
+    def reached(half, part, side):
+        low, high = part * CHUNK, (part + 1) * CHUNK
+        if half == 1 and side == 0:
+            low = max(low, 1)
+        if half == 1 and side == 1:
+            high = min(high, HALF - 1)
+        return low, high - low
+
     def plane_sends(window, n):
-        own = [
-            remote(window.at[pl.ds(near_half, HALF)], window.at[pl.ds(near_half, HALF)], in_send.at[n], in_recv.at[n], at(0, 0, 1)),
-            remote(window.at[pl.ds(near_half, HALF)], window.at[pl.ds(near_half - PLANE, HALF)], in_send.at[n + 1], in_recv.at[n + 1], at(1, 0, 0)),
-            remote(window.at[pl.ds(near_half, HALF)], window.at[pl.ds(near_half + PLANE, HALF)], in_send.at[n + 2], in_recv.at[n + 2], at(3, 0, 0)),
-        ]
-        other = [
-            remote(window.at[pl.ds(other_half, HALF)], window.at[pl.ds(other_half - PLANE, HALF)], in_send.at[n + 3], in_recv.at[n + 3], at(1, 0, 0)),
-            remote(window.at[pl.ds(other_half, HALF)], window.at[pl.ds(other_half + PLANE, HALF)], in_send.at[n + 4], in_recv.at[n + 4], at(3, 0, 0)),
-        ]
-        return own, other
-
-    k_own, k_other = plane_sends(kw, 24)
-    v_own, v_other = plane_sends(vw, 29)
+        to_z, to_y = [], []
+        for part in range(PARTS):
+            span = window.at[pl.ds(near_half + part * CHUNK, CHUNK)]
+            to_z.append(remote(span, span, in_send.at[n], in_recv.at[n], at(0, 0, 1)))
+            n += 1
+        for half, begin in ((1, near_half), (0, other_half)):
+            to_y.append([])
+            for part in range(PARTS):
+                pair = []
+                for side in range(2):
+                    low, count = reached(half, part, side)
+                    src = window.at[pl.ds(begin + low, count)]
+                    dst = window.at[pl.ds(begin + low + (PLANE if side else -PLANE), count)]
+                    pair.append(remote(src, dst, in_send.at[n], in_recv.at[n], at(3 if side else 1, 0, 0)))
+                    n += 1
+                to_y[-1].append(pair)
+        return to_z, to_y[0], to_y[1]
+
+    k_z, k_own, k_other = plane_sends(kw, 24)
+    v_z, v_own, v_other = plane_sends(vw, 24 + 5 * PARTS)
 
     def start(copies):
         for copy in copies:
@@ -138,32 +153,40 @@
         for copy in copies:
             copy.wait()
 
+    def flat(pairs):
+        return [copy for pair in pairs for copy in pair]
+
     q_even, q_odd = q_x[0::OWN], q_x[1::OWN]
-    start(k_x)
+    g_even, g_odd = g_x[0::OWN], g_x[1::OWN]
+    for copies in (k_x, v_x, q_even, q_odd, g_even, g_odd):
+        start(copies)
     dk_acc[...] = jnp.zeros_like(dk_acc)
     dv_acc[...] = jnp.zeros_like(dv_acc)
+    for window in (kw, vw):
+        for end in (z * HALF, 2 * PLANE + z * HALF + HALF - 1):
+            window[end] = jnp.zeros((BLOCK, HD), bf16)
     scale = jnp.concatenate(
         [jnp.full((1, BLOCK), tau_ref[x * PER + h] / math.sqrt(HD), f32) for h in range(PER)], 1
     )
     scale_two = scale * LOG2E
     wait(here_k)
     received(k_x)
-    start(k_own)
-    start(v_x)
-    start(q_even)
+    start(k_z)
+    start(flat(k_own))
     wait(here_v)
     received(v_x)
-    start(v_own)
-    start(q_odd)
-    start(g_x)
-    received(k_own[:1])
-    start(k_other)
-    received(v_own[:1])
-    start(v_other)
+    start(v_z)
+    for part in range(PARTS):
+        received(k_z[part : part + 1])
+        start(k_other[part])
+    start(flat(v_own))
     wait(here_q)
     received(q_even)
-    received(k_own[1:])
-    received(k_other)
+    received(flat(k_own))
+    for part in range(PARTS):
+        received(v_z[part : part + 1])
+        start(v_other[part])
+    received(flat(k_other))
 
     def row_place(r):
         return lax.rem(x - r // OWN + NX, NX) * (NZ * OWN) + z * OWN + lax.rem(r, OWN)
@@ -232,9 +255,9 @@
     received(q_odd)
     lax.fori_loop(0, NX, odd_scores, 0)
     wait(here_g)
-    received(g_x)
-    received(v_own[1:])
-    received(v_other)
+    received(g_even)
+    received(flat(v_own))
+    received(flat(v_other))
 
     def back(r, which, out, local):
         d, half = r // OWN, lax.rem(r, OWN)
@@ -257,7 +280,12 @@
             back(r, which, out, False).start()
 
     def outputs(step, _):
-        r = lax.rem(step + OWN, ROWS)
+        r = lax.rem(step + 1, NX) * OWN + step // NX
+
+        @pl.when(step == NX)
+        def _():
+            received(g_odd)
+
         g = heads_of(g_all, r)
         picks, add = slots(r)
         shift = shift_all[r, 0:1]
@@ -279,7 +307,8 @@
 
     def y_copy(kv, half, part, side):
         n = ((kv * 2 + half) * PARTS + part) * 2 + side
-        return remote(stage.at[n], arrived.at[n], y_send.at[n], y_recv.at[n], at(3 if side == 0 else 1, 0, 0))
+        span = pl.ds(0, reached(half, part, side)[1])
+        return remote(stage.at[n, span], arrived.at[n, span], y_send.at[n], y_recv.at[n], at(3 if side == 0 else 1, 0, 0))
 
     def z_copy(kv, part):
         n = kv * PARTS + part
@@ -305,15 +334,19 @@
         for half in range(2):
             for part in range(PARTS):
                 for side in range(2):
-                    begin = side * 2 * PLANE + (1 - z if half == 0 else z) * HALF + part * CHUNK
-                    stage[((kv * 2 + half) * PARTS + part) * 2 + side] = accs[kv][pl.ds(begin, CHUNK)].astype(bf16)
+                    low, count = reached(half, part, side)
+                    begin = side * 2 * PLANE + (1 - z if half == 0 else z) * HALF + low
+                    n = ((kv * 2 + half) * PARTS + part) * 2 + side
+                    stage[n, :count] = accs[kv][pl.ds(begin, count)].astype(bf16)
                     y_copy(kv, half, part, side).start()
 
     def collected(kv, half, part, begin):
         received(both(kv, half, part))
-        n = ((kv * 2 + half) * PARTS + part) * 2
-        summed = accs[kv][pl.ds(begin + part * CHUNK, CHUNK)]
-        return summed + arrived[n].astype(f32) + arrived[n + 1].astype(f32)
+        for side in range(2):
+            low, count = reached(half, part, side)
+            n = ((kv * 2 + half) * PARTS + part) * 2 + side
+            accs[kv][pl.ds(begin + low, count)] += arrived[n, :count].astype(f32)
+        return accs[kv][pl.ds(begin + part * CHUNK, CHUNK)]
 
     def to_z(kv, part):
         z_stage[kv * PARTS + part] = collected(kv, 0, part, other_half).astype(bf16)
@@ -427,7 +460,7 @@
             for half in range(2):
                 for copy in both(kv, half, part):
                     copy.wait_send()
-    for copy in k_x + v_x + q_x + g_x + k_own + k_other + v_own + v_other + tau_first + tau_second + tau_third:
+    for copy in k_x + v_x + q_x + g_x + k_z + v_z + flat(k_own + k_other + v_own + v_other) + tau_first + tau_second + tau_third:
         copy.wait_send()
 
 
@@ -491,8 +524,8 @@
             pltpu.VMEM((NY, NX, 8, BLOCK), f32),
             pltpu.VMEM((NZ * BATCH, NX, 8, BLOCK), f32),
             pltpu.SemaphoreType.DMA((8,)),
-            pltpu.SemaphoreType.DMA((34,)),
-            pltpu.SemaphoreType.DMA((34,)),
+            pltpu.SemaphoreType.DMA((24 + 10 * PARTS,)),
+            pltpu.SemaphoreType.DMA((24 + 10 * PARTS,)),
             pltpu.SemaphoreType.DMA((2 * ROWS,)),
             pltpu.SemaphoreType.DMA((2 * ROWS,)),
             pltpu.SemaphoreType.DMA((8 * PARTS,)),

time: 90.4 us -> 85.6 us (0.947)
  Pallas kernels: 89.4 us -> 84.8 us
    pallas_call x1, Pallas kernels: 86.8 us -> 82.1 us  [body(): pl.pallas_call(kernel, name='attention', out_shape=(jax.ShapeDtypeStruct(...]
where the time goes in v5:
time: 85.6 us; the launch traced here: 85.4 us
  Pallas kernels  84.8 us (99%)
    pallas_call x1, Pallas kernels, body(): pl.pallas_call(kernel, name='attention', out_shape=(jax.ShapeDtypeStruct(...  82.1 us
    pallas_call x1, Pallas kernels, body(): pl.pallas_call(copy_out, name='copy_out', out_shape=tuple((jax.ShapeDtype...  2.68 us

profile of v5, /device:TPU:0, one launch (start us, length us, event | category | flops | bytes accessed | tf_op | source)
XLA Modules:
  0.0 85.4 jit_solution(2565379900522727839)
XLA Ops:
  0.6 82.1 %attention.1 = (bf16[2,128,2048]{2,1,0:T(8,128)(2,1)}, bf16[2,128,2048]{2,1,0:T(8,128)(2,1)}, bf16[2,128,512]{2,1,0:T(8,128)(2,1)}, bf16[2,128,512]{2,1,0:T(8,128)(2,1)}, f32[16]{0:T(128)}) custom-call(s32[13,4,64]{2,1,0:T(4,128)} %bitcast.13, f32[16]{0:T(128)} %tau_ref.1, bf16[2,128,2048]{2,1,0:T(8,128)(2,1)} %bitcast.9, bf16[2,128,512]{2,1,0:T(8,128)(2,1)} %bitcast.11, ...), custom_call_target="tpu_custom_call" | custom-call | tf_op jit(solution)/shard_map/attention/pallas_call | solution.py:493
  82.7 2.7 %copy_out.1 = (bf16[2,128,2048]{2,1,0:T(8,128)(2,1)}, bf16[2,128,2048]{2,1,0:T(8,128)(2,1)}, bf16[2,128,512]{2,1,0:T(8,128)(2,1)}, bf16[2,128,512]{2,1,0:T(8,128)(2,1)}, f32[16]{0:T(128)}) custom-call(bf16[2,128,2048]{2,1,0:T(8,128)(2,1)} %get-tuple-element.15.refs_0_, bf16[2,128,2048]{2,1,0:T(8,128)(2,1)} %get-tuple-element.16.refs_1_, ...), custom_call_target="tpu_custom_call" | custom-call | tf_op jit(solution)/shard_map/copy_out/pallas_call | solution.py:544

commit v6 on v5

--- a/solution.py
+++ b/solution.py
@@ -188,6 +188,9 @@
         start(v_other[part])
     received(flat(k_other))
 
+    def row_at(step):
+        return lax.rem(ROWS + ROWS // 2 - OWN * lax.rem(step, NX), ROWS) + step // NX
+
     def row_place(r):
         return lax.rem(x - r // OWN + NX, NX) * (NZ * OWN) + z * OWN + lax.rem(r, OWN)
 
@@ -224,8 +227,12 @@
     def heads_of(array, r):
         return jnp.concatenate([array[r, :, h * HD : (h + 1) * HD] for h in range(PER)], 0)
 
-    def folded(array):
-        return array.reshape(BLOCK // 8, 8, WIDE)
+    def folded(array, join):
+        rows = BLOCK
+        while rows > 8:
+            rows //= 2
+            array = join(array[:rows], array[rows:])
+        return array
 
     def scores(r):
         q = heads_of(q_all, r)
@@ -234,12 +241,12 @@
         for k in range(LISTED):
             s = dot(kw[picks[k]], q, 1, 1) * scale_two
             s_all[r, k] = s
-            top = folded(s).max(0)
+            top = folded(s, jnp.maximum)
             high = top if high is None else jnp.maximum(high, top)
         high = high.max(0, keepdims=True)
         total = jnp.zeros((8, WIDE), f32)
         for k in range(LISTED):
-            total = total + folded(jnp.exp2(s_all[r, k] - high)).sum(0)
+            total = total + folded(jnp.exp2(s_all[r, k] - high), jnp.add)
         log_total = jnp.log(total.sum(0, keepdims=True)) * LOG2E
         shift_all[r] = jnp.broadcast_to(high + log_total, (8, WIDE))
 
@@ -280,7 +287,7 @@
             back(r, which, out, False).start()
 
     def outputs(step, _):
-        r = lax.rem(step + 1, NX) * OWN + step // NX
+        r = row_at(step)
 
         @pl.when(step == NX)
         def _():
@@ -374,10 +381,15 @@
     tau_acc[...] = jnp.zeros_like(tau_acc)
 
     def score_grads(step, _):
-        @pl.when(step == 5)
-        def _():
-            for part in range(PARTS):
+        for part in range(PARTS):
+
+            @pl.when(step == 3 + part)
+            def _(part=part):
                 to_z(0, part)
+
+            @pl.when(step == ROWS - PARTS + part)
+            def _(part=part):
+                to_x(0, part)
 
         r = step
         q = heads_of(q_all, r)
@@ -389,7 +401,7 @@
         for k in range(LISTED):
             s = s_all[r, k]
             t = jnp.exp2(s - shift) * (dot(vw[picks[k]], g, 1, 1) - row_dot)
-            tau = tau + folded(t * s).sum(0)
+            tau = tau + folded(t * s, jnp.add)
             ds_all[r, k] = (t * scale).astype(bf16)
         for k in range(LISTED):
             add(dk_acc, k, dot(ds_all[r, k], q, 1, 0))
@@ -405,7 +417,7 @@
     start(tau_first)
 
     def query_grads(step, _):
-        r = lax.rem(step + OWN, ROWS)
+        r = row_at(step)
         picks, _ = slots(r)
         dq = None
         for k in range(LISTED):
@@ -415,16 +427,14 @@
         return 0
 
     lax.fori_loop(0, ROWS // 2, query_grads, 0)
+    received(tau_first)
+    tau_y[y] = tau_x[...]
+    tau_second = [remote(tau_y.at[y], tau_y.at[y], tau_send.at[d + 2], tau_recv.at[d + 2], at(d, 0, 0)) for d in (1, 2, 3)]
+    start(tau_second)
     to_z(1, 0)
     lax.fori_loop(ROWS // 2, ROWS, query_grads, 0)
     for part in range(1, PARTS):
         to_z(1, part)
-    for part in range(PARTS):
-        to_x(0, part)
-    received(tau_first)
-    tau_y[y] = tau_x[...]
-    tau_second = [remote(tau_y.at[y], tau_y.at[y], tau_send.at[d + 2], tau_recv.at[d + 2], at(d, 0, 0)) for d in (1, 2, 3)]
-    start(tau_second)
     received(tau_second)
     spot = z * BATCH + batch
     tau_z[spot] = tau_y[0] + tau_y[1] + tau_y[2] + tau_y[3]

time: 85.6 us -> 83.8 us (0.979)
  Pallas kernels: 84.8 us -> 82.4 us
    pallas_call x1, Pallas kernels: 82.1 us -> 79.7 us  [body(): pl.pallas_call(kernel, name='attention', out_shape=(jax.ShapeDtypeStruct(...]
where the time goes in v6:
time: 83.8 us; the launch traced here: 83.1 us
  Pallas kernels  82.4 us (98%)
    pallas_call x1, Pallas kernels, body(): pl.pallas_call(kernel, name='attention', out_shape=(jax.ShapeDtypeStruct(...  79.7 us
    pallas_call x1, Pallas kernels, body(): pl.pallas_call(copy_out, name='copy_out', out_shape=tuple((jax.ShapeDtype...  2.68 us

profile of v6, /device:TPU:0, one launch (start us, length us, event | category | flops | bytes accessed | tf_op | source)
XLA Modules:
  0.0 83.1 jit_solution(17466184828872665606)
XLA Ops:
  0.6 79.7 %attention.1 = (bf16[2,128,2048]{2,1,0:T(8,128)(2,1)}, bf16[2,128,2048]{2,1,0:T(8,128)(2,1)}, bf16[2,128,512]{2,1,0:T(8,128)(2,1)}, bf16[2,128,512]{2,1,0:T(8,128)(2,1)}, f32[16]{0:T(128)}) custom-call(s32[13,4,64]{2,1,0:T(4,128)} %bitcast.13, f32[16]{0:T(128)} %tau_ref.1, bf16[2,128,2048]{2,1,0:T(8,128)(2,1)} %bitcast.9, bf16[2,128,512]{2,1,0:T(8,128)(2,1)} %bitcast.11, ...), custom_call_target="tpu_custom_call" | custom-call | tf_op jit(solution)/shard_map/attention/pallas_call | solution.py:503
  80.4 2.7 %copy_out.1 = (bf16[2,128,2048]{2,1,0:T(8,128)(2,1)}, bf16[2,128,2048]{2,1,0:T(8,128)(2,1)}, bf16[2,128,512]{2,1,0:T(8,128)(2,1)}, bf16[2,128,512]{2,1,0:T(8,128)(2,1)}, f32[16]{0:T(128)}) custom-call(bf16[2,128,2048]{2,1,0:T(8,128)(2,1)} %get-tuple-element.15.refs_0_, bf16[2,128,2048]{2,1,0:T(8,128)(2,1)} %get-tuple-element.16.refs_1_, ...), custom_call_target="tpu_custom_call" | custom-call | tf_op jit(solution)/shard_map/copy_out/pallas_call | solution.py:554

commit v7 on v6

--- a/solution.py
+++ b/solution.py
@@ -169,6 +169,7 @@
         [jnp.full((1, BLOCK), tau_ref[x * PER + h] / math.sqrt(HD), f32) for h in range(PER)], 1
     )
     scale_two = scale * LOG2E
+    log_scale = jnp.log(scale) * LOG2E
     wait(here_k)
     received(k_x)
     start(k_z)
@@ -274,10 +275,11 @@
             return pltpu.make_async_copy(od.at[r, which], dst, od_recv.at[n])
         return remote(od.at[r, which], dst, od_send.at[n], od_recv.at[n], at(0, NX - d, 0))
 
-    def send_back(r, which, out, result):
+    def put_back(r, which, result):
         for h in range(PER):
             od[r, which, :, h * HD : (h + 1) * HD] = result[h * BLOCK : (h + 1) * BLOCK].astype(bf16)
 
+    def send_back(r, which, out):
         @pl.when(r < OWN)
         def _():
             back(r, which, out, True).start()
@@ -286,13 +288,7 @@
         def _():
             back(r, which, out, False).start()
 
-    def outputs(step, _):
-        r = row_at(step)
-
-        @pl.when(step == NX)
-        def _():
-            received(g_odd)
-
+    def output(r):
         g = heads_of(g_all, r)
         picks, add = slots(r)
         shift = shift_all[r, 0:1]
@@ -302,12 +298,23 @@
             add(dv_acc, k, dot(p, g, 1, 0))
             part = dot(p, vw[picks[k]], 0, 0)
             o = part if o is None else o + part
-        send_back(r, 0, attended, o)
+        put_back(r, 0, o)
         row_dot = (g.astype(f32) * o).sum(-1, keepdims=True)
         dot_all[r] = jnp.broadcast_to(row_dot, (WIDE, HD)).T[0:8]
+
+    def outputs(i, _):
+        @pl.when(i == NX // 2)
+        def _():
+            received(g_odd)
+
+        pair = [row_at(2 * i), row_at(2 * i + 1)]
+        for r in pair:
+            output(r)
+        for r in pair:
+            send_back(r, 0, attended)
         return 0
 
-    lax.fori_loop(0, ROWS, outputs, 0)
+    lax.fori_loop(0, ROWS // 2, outputs, 0)
 
     accs = (dv_acc, dk_acc)
     outs = (value_grad, key_grad)
@@ -396,16 +403,16 @@
         g = heads_of(g_all, r)
         picks, add = slots(r)
         row_dot = dot_all[r, 0:1]
-        shift = shift_all[r, 0:1]
+        shift = shift_all[r, 0:1] - log_scale
         tau = jnp.zeros((8, WIDE), f32)
         for k in range(LISTED):
             s = s_all[r, k]
             t = jnp.exp2(s - shift) * (dot(vw[picks[k]], g, 1, 1) - row_dot)
             tau = tau + folded(t * s, jnp.add)
-            ds_all[r, k] = (t * scale).astype(bf16)
+            ds_all[r, k] = t.astype(bf16)
         for k in range(LISTED):
             add(dk_acc, k, dot(ds_all[r, k], q, 1, 0))
-        tau_acc[...] += tau / scale_two
+        tau_acc[...] += tau / (scale * scale_two)
         return 0
 
     lax.fori_loop(0, ROWS, score_grads, 0)
@@ -423,7 +430,8 @@
         for k in range(LISTED):
             part = dot(ds_all[r, k], kw[picks[k]], 0, 0)
             dq = part if dq is None else dq + part
-        send_back(r, 1, query_grad, dq)
+        put_back(r, 1, dq)
+        send_back(r, 1, query_grad)
         return 0
 
     lax.fori_loop(0, ROWS // 2, query_grads, 0)

time: 83.8 us -> 81.7 us (0.975)
  Pallas kernels: 82.4 us -> 80.8 us
    pallas_call x1, Pallas kernels: 79.7 us -> 78.1 us  [body(): pl.pallas_call(kernel, name='attention', out_shape=(jax.ShapeDtypeStruct(...]
where the time goes in v7:
time: 81.7 us; the launch traced here: 81.4 us
  Pallas kernels  80.8 us (99%)
    pallas_call x1, Pallas kernels, body(): pl.pallas_call(kernel, name='attention', out_shape=(jax.ShapeDtypeStruct(...  78.1 us
    pallas_call x1, Pallas kernels, body(): pl.pallas_call(copy_out, name='copy_out', out_shape=tuple((jax.ShapeDtype...  2.68 us

profile of v7, /device:TPU:0, one launch (start us, length us, event | category | flops | bytes accessed | tf_op | source)
XLA Modules:
  0.0 81.4 jit_solution(1786923436238874280)
XLA Ops:
  0.6 78.1 %attention.1 = (bf16[2,128,2048]{2,1,0:T(8,128)(2,1)}, bf16[2,128,2048]{2,1,0:T(8,128)(2,1)}, bf16[2,128,512]{2,1,0:T(8,128)(2,1)}, bf16[2,128,512]{2,1,0:T(8,128)(2,1)}, f32[16]{0:T(128)}) custom-call(s32[13,4,64]{2,1,0:T(4,128)} %bitcast.13, f32[16]{0:T(128)} %tau_ref.1, bf16[2,128,2048]{2,1,0:T(8,128)(2,1)} %bitcast.9, bf16[2,128,512]{2,1,0:T(8,128)(2,1)} %bitcast.11, ...), custom_call_target="tpu_custom_call" | custom-call | tf_op jit(solution)/shard_map/attention/pallas_call | solution.py:511
  78.8 2.7 %copy_out.1 = (bf16[2,128,2048]{2,1,0:T(8,128)(2,1)}, bf16[2,128,2048]{2,1,0:T(8,128)(2,1)}, bf16[2,128,512]{2,1,0:T(8,128)(2,1)}, bf16[2,128,512]{2,1,0:T(8,128)(2,1)}, f32[16]{0:T(128)}) custom-call(bf16[2,128,2048]{2,1,0:T(8,128)(2,1)} %get-tuple-element.15.refs_0_, bf16[2,128,2048]{2,1,0:T(8,128)(2,1)} %get-tuple-element.16.refs_1_, ...), custom_call_target="tpu_custom_call" | custom-call | tf_op jit(solution)/shard_map/copy_out/pallas_call | solution.py:562

commit v8 on v7

--- a/solution.py
+++ b/solution.py
@@ -22,6 +22,24 @@
 WINDOW = 3 * PLANE
 PARTS = 2
 CHUNK = HALF // PARTS
+REACHED = {
+    (0, 0): (((0, 1), (2, 2)), ((4, 4),)),
+    (0, 1): (((0, 4),), ((4, 2), (7, 1))),
+    (1, 0): (((1, 3),), ((4, 4),)),
+    (1, 1): (((0, 4),), ((4, 3),)),
+}
+PIECES = [
+    (half, part, side, low, count)
+    for half in range(2)
+    for part in range(PARTS)
+    for side in range(2)
+    for low, count in REACHED[half, side][part]
+]
+
+
+def pieces(half, part):
+    return [(n, p[2], p[3], p[4]) for n, p in enumerate(PIECES) if p[:2] == (half, part)]
+
 TOKENS = OWN * BLOCK
 FIXED = (-1, 0, 1, 6, -6)
 EITHER = ((2, 3), (-2, -3), (4, 9), (-4, -9), (8, 12), (-8, -12), (10, 15), (-10, -15))
@@ -111,14 +129,6 @@
     q_x = along_x(queries, WIDE, lambda d, n: q_all.at[d * OWN + n], 12)
     g_x = along_x(grads, WIDE, lambda d, n: g_all.at[d * OWN + n], 18)
 
-    def reached(half, part, side):
-        low, high = part * CHUNK, (part + 1) * CHUNK
-        if half == 1 and side == 0:
-            low = max(low, 1)
-        if half == 1 and side == 1:
-            high = min(high, HALF - 1)
-        return low, high - low
-
     def plane_sends(window, n):
         to_z, to_y = [], []
         for part in range(PARTS):
@@ -129,8 +139,7 @@
             to_y.append([])
             for part in range(PARTS):
                 pair = []
-                for side in range(2):
-                    low, count = reached(half, part, side)
+                for _, side, low, count in pieces(half, part):
                     src = window.at[pl.ds(begin + low, count)]
                     dst = window.at[pl.ds(begin + low + (PLANE if side else -PLANE), count)]
                     pair.append(remote(src, dst, in_send.at[n], in_recv.at[n], at(3 if side else 1, 0, 0)))
@@ -139,7 +148,7 @@
         return to_z, to_y[0], to_y[1]
 
     k_z, k_own, k_other = plane_sends(kw, 24)
-    v_z, v_own, v_other = plane_sends(vw, 24 + 5 * PARTS)
+    v_z, v_own, v_other = plane_sends(vw, 24 + PARTS + len(PIECES))
 
     def start(copies):
         for copy in copies:
@@ -163,7 +172,10 @@
     dk_acc[...] = jnp.zeros_like(dk_acc)
     dv_acc[...] = jnp.zeros_like(dv_acc)
     for window in (kw, vw):
-        for end in (z * HALF, 2 * PLANE + z * HALF + HALF - 1):
+        for end in (
+            z * HALF, 2 * PLANE + z * HALF + HALF - 1,
+            (1 - z) * HALF + 1, 2 * PLANE + (1 - z) * HALF + 6,
+        ):
             window[end] = jnp.zeros((BLOCK, HD), bf16)
     scale = jnp.concatenate(
         [jnp.full((1, BLOCK), tau_ref[x * PER + h] / math.sqrt(HD), f32) for h in range(PER)], 1
@@ -319,10 +331,15 @@
     accs = (dv_acc, dk_acc)
     outs = (value_grad, key_grad)
 
-    def y_copy(kv, half, part, side):
-        n = ((kv * 2 + half) * PARTS + part) * 2 + side
-        span = pl.ds(0, reached(half, part, side)[1])
-        return remote(stage.at[n, span], arrived.at[n, span], y_send.at[n], y_recv.at[n], at(3 if side == 0 else 1, 0, 0))
+    def held(kv, piece):
+        half, part, side, low, _ = PIECES[piece]
+        return ((kv * 2 + half) * PARTS + part) * 2 + side, low - part * CHUNK
+
+    def y_copy(kv, piece, side, count):
+        n = kv * len(PIECES) + piece
+        slot, first = held(kv, piece)
+        span = pl.ds(first, count)
+        return remote(stage.at[slot, span], arrived.at[slot, span], y_send.at[n], y_recv.at[n], at(3 if side == 0 else 1, 0, 0))
 
     def z_copy(kv, part):
         n = kv * PARTS + part
@@ -342,24 +359,20 @@
         return remote(final.at[kv, m], dst, x_send.at[n], x_recv.at[n], at(0, d, 0))
 
     def both(kv, half, part):
-        return [y_copy(kv, half, part, side) for side in range(2)]
+        return [y_copy(kv, n, side, count) for n, side, _, count in pieces(half, part)]
 
     def to_y(kv):
-        for half in range(2):
-            for part in range(PARTS):
-                for side in range(2):
-                    low, count = reached(half, part, side)
-                    begin = side * 2 * PLANE + (1 - z if half == 0 else z) * HALF + low
-                    n = ((kv * 2 + half) * PARTS + part) * 2 + side
-                    stage[n, :count] = accs[kv][pl.ds(begin, count)].astype(bf16)
-                    y_copy(kv, half, part, side).start()
+        for n, (half, part, side, low, count) in enumerate(PIECES):
+            begin = side * 2 * PLANE + (1 - z if half == 0 else z) * HALF + low
+            slot, first = held(kv, n)
+            stage[slot, first : first + count] = accs[kv][pl.ds(begin, count)].astype(bf16)
+            y_copy(kv, n, side, count).start()
 
     def collected(kv, half, part, begin):
         received(both(kv, half, part))
-        for side in range(2):
-            low, count = reached(half, part, side)
-            n = ((kv * 2 + half) * PARTS + part) * 2 + side
-            accs[kv][pl.ds(begin + low, count)] += arrived[n, :count].astype(f32)
+        for n, side, low, count in pieces(half, part):
+            slot, first = held(kv, n)
+            accs[kv][pl.ds(begin + low, count)] += arrived[slot, first : first + count].astype(f32)
         return accs[kv][pl.ds(begin + part * CHUNK, CHUNK)]
 
     def to_z(kv, part):
@@ -423,24 +436,26 @@
     tau_first = [remote(tau_x.at[x], tau_x.at[x], tau_send.at[d - 1], tau_recv.at[d - 1], at(0, d, 0)) for d in (1, 2, 3)]
     start(tau_first)
 
-    def query_grads(step, _):
-        r = row_at(step)
-        picks, _ = slots(r)
-        dq = None
-        for k in range(LISTED):
-            part = dot(ds_all[r, k], kw[picks[k]], 0, 0)
-            dq = part if dq is None else dq + part
-        put_back(r, 1, dq)
-        send_back(r, 1, query_grad)
+    def query_grads(i, _):
+        pair = [row_at(2 * i), row_at(2 * i + 1)]
+        for r in pair:
+            picks, _ = slots(r)
+            dq = None
+            for k in range(LISTED):
+                part = dot(ds_all[r, k], kw[picks[k]], 0, 0)
+                dq = part if dq is None else dq + part
+            put_back(r, 1, dq)
+        for r in pair:
+            send_back(r, 1, query_grad)
         return 0
 
-    lax.fori_loop(0, ROWS // 2, query_grads, 0)
+    lax.fori_loop(0, ROWS // 4, query_grads, 0)
     received(tau_first)
     tau_y[y] = tau_x[...]
     tau_second = [remote(tau_y.at[y], tau_y.at[y], tau_send.at[d + 2], tau_recv.at[d + 2], at(d, 0, 0)) for d in (1, 2, 3)]
     start(tau_second)
     to_z(1, 0)
-    lax.fori_loop(ROWS // 2, ROWS, query_grads, 0)
+    lax.fori_loop(ROWS // 4, ROWS // 2, query_grads, 0)
     for part in range(1, PARTS):
         to_z(1, part)
     received(tau_second)
@@ -542,12 +557,12 @@
             pltpu.VMEM((NY, NX, 8, BLOCK), f32),
             pltpu.VMEM((NZ * BATCH, NX, 8, BLOCK), f32),
             pltpu.SemaphoreType.DMA((8,)),
-            pltpu.SemaphoreType.DMA((24 + 10 * PARTS,)),
-            pltpu.SemaphoreType.DMA((24 + 10 * PARTS,)),
+            pltpu.SemaphoreType.DMA((24 + 2 * PARTS + 2 * len(PIECES),)),
+            pltpu.SemaphoreType.DMA((24 + 2 * PARTS + 2 * len(PIECES),)),
             pltpu.SemaphoreType.DMA((2 * ROWS,)),
             pltpu.SemaphoreType.DMA((2 * ROWS,)),
-            pltpu.SemaphoreType.DMA((8 * PARTS,)),
-            pltpu.SemaphoreType.DMA((8 * PARTS,)),
+            pltpu.SemaphoreType.DMA((2 * len(PIECES),)),
+            pltpu.SemaphoreType.DMA((2 * len(PIECES),)),
             pltpu.SemaphoreType.DMA((2 * PARTS,)),
             pltpu.SemaphoreType.DMA((2 * PARTS,)),
             pltpu.SemaphoreType.DMA((2 * NX * OWN,)),

time: 81.7 us -> 80.4 us (0.984)
  Pallas kernels: 80.8 us -> 79.5 us
    pallas_call x1, Pallas kernels: 78.1 us -> 76.8 us  [body(): pl.pallas_call(kernel, name='attention', out_shape=(jax.ShapeDtypeStruct(...]
where the time goes in v8:
time: 80.4 us; the launch traced here: 80.1 us
  Pallas kernels  79.5 us (99%)
    pallas_call x1, Pallas kernels, body(): pl.pallas_call(kernel, name='attention', out_shape=(jax.ShapeDtypeStruct(...  76.8 us
    pallas_call x1, Pallas kernels, body(): pl.pallas_call(copy_out, name='copy_out', out_shape=tuple((jax.ShapeDtype...  2.68 us

profile of v8, /device:TPU:0, one launch (start us, length us, event | category | flops | bytes accessed | tf_op | source)
XLA Modules:
  0.0 80.1 jit_solution(17001825015431838763)
XLA Ops:
  0.6 76.8 %attention.1 = (bf16[2,128,2048]{2,1,0:T(8,128)(2,1)}, bf16[2,128,2048]{2,1,0:T(8,128)(2,1)}, bf16[2,128,512]{2,1,0:T(8,128)(2,1)}, bf16[2,128,512]{2,1,0:T(8,128)(2,1)}, f32[16]{0:T(128)}) custom-call(s32[13,4,64]{2,1,0:T(4,128)} %bitcast.13, f32[16]{0:T(128)} %tau_ref.1, bf16[2,128,2048]{2,1,0:T(8,128)(2,1)} %bitcast.9, bf16[2,128,512]{2,1,0:T(8,128)(2,1)} %bitcast.11, ...), custom_call_target="tpu_custom_call" | custom-call | tf_op jit(solution)/shard_map/attention/pallas_call | solution.py:526
  77.5 2.7 %copy_out.1 = (bf16[2,128,2048]{2,1,0:T(8,128)(2,1)}, bf16[2,128,2048]{2,1,0:T(8,128)(2,1)}, bf16[2,128,512]{2,1,0:T(8,128)(2,1)}, bf16[2,128,512]{2,1,0:T(8,128)(2,1)}, f32[16]{0:T(128)}) custom-call(bf16[2,128,2048]{2,1,0:T(8,128)(2,1)} %get-tuple-element.15.refs_0_, bf16[2,128,2048]{2,1,0:T(8,128)(2,1)} %get-tuple-element.16.refs_1_, ...), custom_call_target="tpu_custom_call" | custom-call | tf_op jit(solution)/shard_map/copy_out/pallas_call | solution.py:577
